TPU v7x, 256 devices: a whole 4x4x8 slice. The times are simulated.
256 devices in a mesh: ctx: 32 (over y, z), tp: 8 (over x, core).
Axes of the slice: x: 4, y: 4, z: 8, core: 2. Of those that a mesh axis runs over, the one named last changes fastest.
Arguments:
- prompt_states: bfloat16 [16384, 5376], P('ctx', 'tp'), may hold values from -400 to 400
- decode_states: bfloat16 [512, 5376], P('ctx', 'tp'), may hold values from -400 to 400
- norm_gain: float32 [5376], replicated, may hold values from 0.25 to 1.75
- query_weight: bfloat16 [5376, 4096], P(None, 'tp'), may hold values from -0.078125 to 0.078125
- key_weight: bfloat16 [5376, 2048], P(None, 'tp'), may hold values from -0.078125 to 0.078125
- value_weight: bfloat16 [5376, 2048], P(None, 'tp'), may hold values from -0.078125 to 0.078125
- query_gain: float32 [128], replicated, may hold values from 1 to 20
- key_gain: float32 [128], replicated, may hold values from 1 to 20
- prompt_lengths: int32 [4], replicated, may hold values from 2049 to 4096, as said below
- row_prompt: int32 [512], P('ctx'), may hold values from 0 to 3
Outputs:
- prefill_attention: bfloat16 [16384, 4096], P('ctx', 'tp')
- decode_attention: bfloat16 [512, 4096], P('ctx', 'tp')
Inputs may be any that keep to these rules, and one draw needn't show every extreme that they name: `prompt_lengths`: every prompt has more than half of its 4096 slots live and one prompt fills all of them.
All inputs are finite; a program needn't handle non-finite values.
Results may differ from a plain program's by a relative error of at most 0.02.
The roundings to bfloat16 on the way count: a program that leaves them out, or rounds other values in their place, can miss the bound.
Values may be sent and summed in bfloat16 or wider, within the bound.
A program may use at most 128 MiB of HBM per device.

v0:
```python
import jax
import jax.numpy as jnp
from jax import lax
from jax.sharding import PartitionSpec as P

WINDOW = 1024
PROMPTS = 4


EPS = 1e-06
SCORE_SCALE = 168.0 ** (-0.5)


def shifted(value, axis, steps):
    count = lax.axis_size(axis)
    initial, last = (max(0, -steps), min(count, count - steps))
    return lax.ppermute(value, axis, [(source, source + steps) for source in range(initial, last)])


def rotate(vectors, positions):
    half_size = vectors.shape[-1] // 2
    frequency = 10000.0 ** (-(jnp.arange(half_size, dtype=jnp.float32) * 2.0) / vectors.shape[-1])
    angles = positions.astype(jnp.float32)[:, None, None] * frequency
    cosine = jnp.cos(angles)
    sine_part = jnp.sin(angles)
    first_half = vectors[..., :half_size]
    second_half = vectors[..., half_size:]
    return jnp.concatenate(
        [
            first_half * cosine - second_half * sine_part,
            second_half * cosine + first_half * sine_part,
        ],
        axis=-1,
    )


def head_norm(vectors, gain_values):
    return (
        vectors * lax.rsqrt(jnp.mean(vectors * vectors, axis=-1, keepdims=True) + EPS) * gain_values
    )


def finish(sums, query_acc, key_acc, value_acc, positions, feature_count, query_gain, key_gain):
    row_count = sums.shape[0]
    head_size = query_gain.shape[0]
    inverse = lax.rsqrt(sums / feature_count + EPS)[:, None]
    query_heads = rotate(
        head_norm((query_acc * inverse).reshape(row_count, -1, head_size), query_gain), positions
    ).astype(jnp.bfloat16)
    key_heads = rotate(
        head_norm((key_acc * inverse).reshape(row_count, -1, head_size), key_gain), positions
    ).astype(jnp.bfloat16)
    value_heads = (value_acc * inverse).reshape(row_count, -1, head_size).astype(jnp.bfloat16)
    return (query_heads, key_heads, value_heads)


def window_mask(query_index, key_index, slot_size):
    later = key_index[None, :]
    earlier = query_index[:, None]
    return (
        (later >= 0)
        & (later // slot_size == earlier // slot_size)
        & (later <= earlier)
        & (later > earlier - WINDOW)
    )


def local(
    prompt_states,
    decode_states,
    norm_gain,
    query_weight,
    key_weight,
    value_weight,
    query_gain,
    key_gain,
    prompt_lengths,
    row_prompt,
):
    tok_rows = prompt_states.shape[0]
    dec_rows = decode_states.shape[0]
    feature_count = norm_gain.shape[0]
    shards = lax.axis_size("ctx")
    my_index = lax.axis_index("ctx")
    slot_size = tok_rows * shards // PROMPTS
    query_cols = query_weight.shape[1]
    kv_cols = key_weight.shape[1]
    initial = (
        jnp.zeros((tok_rows,), jnp.float32),
        jnp.zeros((tok_rows, query_cols), jnp.float32),
        jnp.zeros((tok_rows, kv_cols), jnp.float32),
        jnp.zeros((tok_rows, kv_cols), jnp.float32),
        jnp.zeros((dec_rows,), jnp.float32),
        jnp.zeros((dec_rows, query_cols), jnp.float32),
        jnp.zeros((dec_rows, kv_cols), jnp.float32),
        jnp.zeros((dec_rows, kv_cols), jnp.float32),
    )

    def advance(states, sums, query_acc, key_acc, value_acc):
        widened = states.astype(jnp.float32)
        scaled = (widened * norm_gain).astype(jnp.bfloat16)
        return (
            jnp.sum(widened * widened, axis=1),
            jnp.dot(scaled, query_weight, preferred_element_type=jnp.float32),
            jnp.dot(scaled, key_weight, preferred_element_type=jnp.float32),
            jnp.dot(scaled, value_weight, preferred_element_type=jnp.float32),
        )

    folded = advance(
        lax.all_gather(prompt_states, "tp", axis=1, tiled=True), *initial[:4]
    ) + advance(lax.all_gather(decode_states, "tp", axis=1, tiled=True), *initial[4:])
    my_prompt = my_index % PROMPTS
    my_block = my_index // PROMPTS
    positions = my_block * tok_rows + jnp.arange(tok_rows, dtype=jnp.int32)
    query_index = my_prompt * slot_size + positions
    query_heads, key_heads, value_heads = finish(
        folded[0], folded[1], folded[2], folded[3], positions, feature_count, query_gain, key_gain
    )
    send_rows = min(tok_rows, WINDOW)
    halo_depth = WINDOW // send_rows
    arrived = [
        shifted((key_heads, value_heads), "ctx", hop_count * PROMPTS)
        for hop_count in range(halo_depth, 0, -1)
    ]
    ext_keys = jnp.concatenate([arrival[0] for arrival in arrived] + [key_heads], axis=0)
    ext_values = jnp.concatenate([arrival[1] for arrival in arrived] + [value_heads], axis=0)
    kv_local = key_heads.shape[1]
    group_size = query_heads.shape[1] // kv_local
    head_size = query_gain.shape[0]
    grouped = query_heads.reshape(tok_rows, kv_local, group_size, head_size)
    scores = (
        jnp.einsum("tkgd,skd->kgts", grouped, ext_keys, preferred_element_type=jnp.float32)
        * SCORE_SCALE
    )
    key_index = (
        my_prompt * slot_size
        + my_block * tok_rows
        - WINDOW
        + jnp.arange(WINDOW + tok_rows, dtype=jnp.int32)
    )
    visible = window_mask(query_index, key_index, slot_size)
    row_top = jnp.max(jnp.where(visible, scores, -jnp.inf), axis=-1, keepdims=True)
    weights = jnp.where(visible, jnp.exp(scores - row_top), 0.0)
    weight_sum = jnp.sum(weights, axis=-1)
    mixture = jnp.einsum(
        "kgts,skd->tkgd",
        weights.astype(jnp.bfloat16),
        ext_values,
        preferred_element_type=jnp.float32,
    )
    mixture = mixture / jnp.transpose(weight_sum, (2, 0, 1))[..., None]
    my_length = jnp.sum(
        jnp.where(jnp.arange(PROMPTS, dtype=jnp.int32) == my_prompt, prompt_lengths, 0)
    )
    alive_rows = positions < my_length
    prefill_attention = (
        jnp.where(alive_rows[:, None, None, None], mixture, 0.0)
        .astype(jnp.bfloat16)
        .reshape(tok_rows, -1)
    )
    last_shard = (prompt_lengths - 1) // tok_rows * PROMPTS + jnp.arange(PROMPTS, dtype=jnp.int32)
    offsets = (prompt_lengths - 1) % tok_rows + 1
    decode_match = row_prompt[:, None] == jnp.arange(PROMPTS, dtype=jnp.int32)[None, :]
    decode_lengths = jnp.sum(jnp.where(decode_match, prompt_lengths[None, :], 0), axis=1)
    decode_query, decode_keys, decode_values = finish(
        folded[4],
        folded[5],
        folded[6],
        folded[7],
        decode_lengths,
        feature_count,
        query_gain,
        key_gain,
    )
    local_keys = jax.vmap(lambda offset: lax.dynamic_slice_in_dim(ext_keys, offset, WINDOW, 0))(
        offsets
    )
    local_values = jax.vmap(lambda offset: lax.dynamic_slice_in_dim(ext_values, offset, WINDOW, 0))(
        offsets
    )
    owner = (last_shard == my_index)[:, None, None, None]
    zero_value = jnp.zeros((), jnp.bfloat16)
    summed = (
        lax.psum(jnp.where(owner, local_keys, zero_value), "ctx").astype(jnp.float32),
        lax.psum(jnp.where(owner, local_values, zero_value), "ctx").astype(jnp.float32),
    )
    tail_keys = summed[0].astype(jnp.bfloat16)
    tail_values = summed[1].astype(jnp.bfloat16)
    decode_grouped = decode_query.reshape(dec_rows, kv_local, group_size, head_size)
    tail_scores = (
        jnp.einsum(
            "rkgd,pwkd->rkgpw", decode_grouped, tail_keys, preferred_element_type=jnp.float32
        )
        * SCORE_SCALE
    )
    own_scores = (
        jnp.einsum("rkgd,rkd->rkg", decode_grouped, decode_keys, preferred_element_type=jnp.float32)
        * SCORE_SCALE
    )
    chosen = decode_match[:, None, None, :, None]
    decode_top = jnp.maximum(
        jnp.max(jnp.where(chosen, tail_scores, -jnp.inf), axis=(3, 4)), own_scores
    )
    tail_weights = jnp.where(chosen, jnp.exp(tail_scores - decode_top[..., None, None]), 0.0)
    own_weights = jnp.exp(own_scores - decode_top)
    decode_sum = jnp.sum(tail_weights, axis=(3, 4)) + own_weights
    decode_mix = jnp.einsum(
        "rkgpw,pwkd->rkgd",
        tail_weights.astype(jnp.bfloat16),
        tail_values,
        preferred_element_type=jnp.float32,
    )
    decode_mix = (
        decode_mix
        + own_weights.astype(jnp.bfloat16).astype(jnp.float32)[..., None]
        * decode_values.astype(jnp.float32)[:, :, None, :]
    )
    decode_attention = (
        (decode_mix / decode_sum[..., None]).astype(jnp.bfloat16).reshape(dec_rows, -1)
    )
    return (prefill_attention, decode_attention)


def solution(mesh):
    placed = (
        P("ctx", "tp"),
        P("ctx", "tp"),
        P(),
        P(None, "tp"),
        P(None, "tp"),
        P(None, "tp"),
        P(),
        P(),
        P(),
        P("ctx"),
    )
    return jax.shard_map(
        local,
        mesh=mesh,
        in_specs=placed,
        out_specs=(P("ctx", "tp"), P("ctx", "tp")),
        check_vma=False,
    )
```

profile of v0, /device:TPU:1, one launch (start us, length us, event | category | flops | bytes accessed | tf_op | source)
XLA Modules:
  0.0 302.0 jit_solution(5375320829911485615)
XLA Ops:
  10.8 16.0 %all-gather = bf16[8,672,16]{1,2,0:T(8,128)(2,1)S(1)} all-gather(bf16[1,672,16]{1,2,0:T(8,128)(2,1)} %bitcast.168), channel_id=1, replica_groups=mesh['ctx'=32,'tp'=8] {'tp'}, dimensions={0}, use_global_device_ids=true | all-gather | bytes 193536 | tf_op jit(solution)/shard_map/all_gather | solution.py:111
  27.9 2.2 fusion.51
  30.8 3.4 %convolution_multiply_fusion.3 = f32[16,512]{1,0:T(8,128)S(1)} fusion(bf16[5376,16]{0,1:T(8,128)(2,1)S(1)} %get-tuple-element.81, bf16[5376,512]{1,0:T(8,128)(2,1)} %param.13, f32[16]{0:T(128)S(1)} %add_rsqrt_fusion.5), kind=kOutput, calls=%fused_computation.41 | convolution fusion | flops 88088576 | bytes 5709888 | tf_op jit(solution)/shard_map/dot_general | solution.py:104
  42.3 11.8 %all-gather.3.cloned.1.call-done = bf16[512,5376]{0,1:T(8,128)(2,1)} async-done(((bf16[512,672]{0,1:T(8,128)(2,1)}), bf16[512,5376]{0,1:T(8,128)(2,1)}) %all-gather.3.cloned.1.call-update) | async-done | bytes 5505040 | tf_op jit(solution)/shard_map/all_gather | solution.py:110
  54.1 3.9 %fusion.6 = f32[512]{0:T(512)S(1)} fusion(bf16[512,5376]{0,1:T(8,128)(2,1)} %all-gather.3.cloned.1.call-done), kind=kLoop, calls=%fused_computation.17 | loop fusion | flops 8257024 | bytes 5507072 | tf_op jit(solution)/shard_map/reduce_sum | solution.py:103
  58.3 2.7 multiply_reduce_fusion.1
  65.3 7.4 %collective-permute-start.3 = (bf16[512,2,128]{2,0,1:T(8,128)(2,1)S(1)}, bf16[512,2,128]{2,0,1:T(8,128)(2,1)S(1)}, u32[]{:S(2)}, u32[]{:S(2)}) collective-permute-start(bf16[512,2,128]{2,0,1:T(8,128)(2,1)S(1)} %pad_maximum_fusion.2), channel_id=1, source_target_pairs={{0,32},{8,40},{16,48},{24,56},{32,64},{40,72},{48,80},{56,88},{64,... | collective-permute-start | bytes 786440 | tf_op jit(solution)/shard_map/ppermute | solution.py:17
  72.7 3.1 %collective-permute-start.2 = (bf16[512,2,128]{2,0,1:T(8,128)(2,1)S(1)}, bf16[512,2,128]{2,0,1:T(8,128)(2,1)S(1)}, u32[]{:S(2)}, u32[]{:S(2)}) collective-permute-start(bf16[512,2,128]{2,0,1:T(8,128)(2,1)S(1)} %pad_maximum_fusion.2), channel_id=1, source_target_pairs={{0,64},{8,72},{16,80},{24,88},{32,96},{40,104},{48,112},{56,120},{... | collective-permute-start | bytes 786440 | tf_op jit(solution)/shard_map/ppermute | solution.py:17
  75.8 5.2 %fusion.36 = bf16[512,256]{0,1:T(8,128)(2,1)} fusion(bf16[5376,256]{1,0:T(8,128)(2,1)S(1)} %copy-done.4, f32[512]{0:T(512)S(1)} %copy-done.25, bf16[512,5376]{0,1:T(8,128)(2,1)} %all-gather.3.cloned.1.call-done, f32[5376]{0:T(1024)S(1)} %copy-done.12), kind=kOutput, calls=%fused_computation.40 | convolution fusion | flops 1417805824 | bytes 8543232 | tf_op jit(solution)/shard_map/dot_general | solution.py:106
  81.0 3.5 %collective-permute-start.1 = (bf16[512,2,128]{0,2,1:T(8,128)(2,1)}, bf16[512,2,128]{0,2,1:T(8,128)(2,1)}, u32[]{:S(2)}, u32[]{:S(2)}) collective-permute-start(bf16[512,2,128]{0,2,1:T(8,128)(2,1)} %bitcast), channel_id=1, source_target_pairs={{0,32},{8,40},{16,48},{24,56},{32,64},{40,72},{48,80},{56,88},{64,... | collective-permute-start | bytes 786440 | tf_op jit(solution)/shard_map/ppermute | solution.py:17
  84.5 2.8 collective-permute-start
  87.5 1.6 broadcast.351.clone3
  89.1 9.2 %while.3 = (s32[]{:T(128)}, bf16[1536,2,128]{2,0,1:T(8,128)(2,1)S(1)}, s32[4,3]{1,0:T(4,128)}, bf16[4,1024,2,128]{3,1,0,2:T(8,128)(2,1)}, s32[]{:T(128)}) while((s32[]{:T(128)}, bf16[1536,2,128]{2,0,1:T(8,128)(2,1)S(1)}, s32[4,3]{1,0:T(4,128)}, bf16[4,1024,2,128]{3,1,0,2:T(8,128)(2,1)}, s32[]{:T(128)}) %tuple.60), condition=%wide.while_cond.1, body=%wide.while_body.1.sunk | while | flops 2 | bytes 3145833 | solution.py:175
  98.2 2.4 pad_maximum_fusion
  100.6 1.6 broadcast.351.clone3.1
  102.2 19.9 %while.2 = (s32[]{:T(128)}, bf16[1536,2,128]{0,2,1:T(8,128)(2,1)}, s32[4,3]{1,0:T(4,128)}, bf16[4,1024,2,128]{3,1,0,2:T(8,128)(2,1)}, s32[]{:T(128)}) while((s32[]{:T(128)}, bf16[1536,2,128]{0,2,1:T(8,128)(2,1)}, s32[4,3]{1,0:T(4,128)}, bf16[4,1024,2,128]{3,1,0,2:T(8,128)(2,1)}, s32[]{:T(128)}) %tuple.71), condition=%wide.while_cond, body=%wide.while_body.sunk | while | flops 2 | bytes 3145833 | solution.py:178
  102.9 2.1 constant_dynamic-slice_fusion.9
  105.0 1.3 copy.127
  107.9 2.1 constant_dynamic-slice_fusion.9
  110.0 1.3 copy.127
  112.9 2.1 constant_dynamic-slice_fusion.9
  115.0 1.3 copy.127
  117.8 2.1 constant_dynamic-slice_fusion.9
  122.1 4.6 %broadcast_select_fusion = (bf16[4,1024,2,128]{3,1,0,2:T(8,128)(2,1)}, bf16[4,1024,2,128]{3,1,0,2:T(8,128)(2,1)}) fusion(bf16[4,1024,2,128]{3,1,0,2:T(8,128)(2,1)} %get-tuple-element.17, pred[4]{0:T(512)(128)(4,1)} %add_compare_fusion, bf16[4,1024,2,128]{3,1,0,2:T(8,128)(2,1)} %get-tuple-element.9), kind=kLoop, calls=%fused_computation.28 | loop fusion | flops 2097152 | bytes 8388612 | tf_op jit(solution)/shard_map/jit(_where)/select_n | solution.py:184
  128.0 2.6 compare_and_fusion
  130.6 7.7 %multiply_reduce_fusion = (f32[512,4]{0,1:T(4,128)S(1)}, f32[512,512]{0,1:T(8,128)S(1)}) fusion(f32[512]{0:T(512)S(1)} %copy-done.26, bf16[5376,512]{1,0:T(8,128)(2,1)} %param.13, bf16[512,5376]{0,1:T(8,128)(2,1)} %all-gather.3.cloned.1.call-done, f32[5376]{0:T(1024)S(1)} %copy-done.13), kind=kOutput, calls=%fused_computation.54 | convolution fusion | flops 2827614208 | bytes 12090368 | tf_op jit(solution)/shard_map/dot_general | solution.py:104
  139.5 2.0 copy.76
  141.5 2.0 copy.77
  143.4 9.5 %fusion.95 = (f32[2,2,512]{2,1,0:T(2,128)}, bf16[2,2,512,1536]{2,3,1,0:T(8,128)(2,1)}) fusion(pred[512,1536]{0,1:T(8,128)(4,1)} %compare_and_fusion, bf16[1536,2,128]{2,0,1:T(8,128)(2,1)S(1)} %copy-done.2, bf16[512,2,2,64]{3,0,2,1:T(8,128)(2,1)} %bitcast.163, bf16[512,2,2,64]{3,0,2,1:T(8,128)(2,1)} %bitcast.162), kind=kOutput, calls=%fused_computation.148 | convolution fusion | flops 1634731520 | bytes 8396800 | tf_op jit(solution)/shard_map/sub | solution.py:143
  153.0 4.1 %fusion.33 = bf16[512,2,2,128]{0,3,2,1:T(8,128)(2,1)S(1)} fusion(bf16[2,2,512,1536]{2,3,1,0:T(8,128)(2,1)} %get-tuple-element.101, f32[512,2,2]{0,2,1:T(2,128)} %bitcast.172, pred[512]{0:T(512)(128)(4,1)} %fusion.77, bf16[512,2,128]{0,2,1:T(8,128)(2,1)} %bitcast, bf16[512,2,128]{0,2,1:T(8,128)(2,1)} %collective-permute-done.1, ...), kind=kOutput, calls=%fused_computation.37 | convolution fusion | flops 808452096 | bytes 7610880 | tf_op jit(solution)/shard_map/kgts,skd->tkgd/dot_general | solution.py:145
  158.1 132.8 %all-reduce.4.cloned.1.call-done = (bf16[4,1024,2,128]{3,1,0,2:T(8,128)(2,1)}, bf16[4,1024,2,128]{3,1,0,2:T(8,128)(2,1)}) async-done(((bf16[4,1024,2,128]{3,1,0,2:T(8,128)(2,1)}, bf16[4,1024,2,128]{3,1,0,2:T(8,128)(2,1)}), (bf16[4,1024,2,128]{3,1,0,2:T(8,128)(2,1)}, bf16[4,1024,2,128]{3,1,0,2:T(8,128)(2,1)})) %all-reduce.4.cloned.1.call-update) | async-done | bytes 4194320 | tf_op jit(solution)/shard_map/psum | solution.py:185
  290.9 2.6 select_reduce_fusion
  (150 shorter events, 39.3 us)
Async XLA Ops:
  7.2 27.2 %copy-start = (bf16[5376,256]{1,0:T(8,128)(2,1)S(1)}, bf16[5376,256]{1,0:T(8,128)(2,1)}, u32[]{:S(2)}) copy-start(bf16[5376,256]{1,0:T(8,128)(2,1)} %param.14) | copy-start | bytes 8257540
  7.2 46.9 %all-gather.3.cloned.1.call-start = ((), (), s32[]{:S(2)}) async-start(), calls=%async_computation | async-start | bytes 6193152 | tf_op jit(solution)/shard_map/all_gather | solution.py:110
  7.9 283.0 %all-reduce.4.cloned.1.call-start = ((), (), s32[]{:S(2)}) async-start(), calls=%async_computation.1 | async-start | bytes 8388608 | tf_op jit(solution)/shard_map/psum | solution.py:185
  34.3 7.4 %copy-start.27 = (s32[4]{0:T(128)S(1)}, s32[4]{0:T(128)}, u32[]{:S(2)}) copy-start(s32[4]{0:T(128)} %param.18) | copy-start | bytes 52
  37.2 20.9 %copy-start.5 = (f32[512,64]{0,1:T(8,128)}, f32[512,64]{0,1:T(8,128)S(1)}, u32[]{:S(2)}) copy-start(f32[512,64]{0,1:T(8,128)S(1)} %get-tuple-element.88) | copy-start | bytes 393220
  37.2 20.9 %copy-start.7 = (f32[512,64]{0,1:T(8,128)}, f32[512,64]{0,1:T(8,128)S(1)}, u32[]{:S(2)}) copy-start(f32[512,64]{0,1:T(8,128)S(1)} %get-tuple-element.89) | copy-start | bytes 393220
  37.3 20.8 %copy-start.11 = (f32[5376]{0:T(1024)S(1)}, f32[5376]{0:T(1024)}, u32[]{:S(2)}) copy-start(f32[5376]{0:T(1024)} %param.12) | copy-start | bytes 64516
  54.1 4.2 %copy-start.3 = (bf16[512,5376]{0,1:T(8,128)(2,1)S(1)}, bf16[512,5376]{0,1:T(8,128)(2,1)}, u32[]{:S(2)}) copy-start(bf16[512,5376]{0,1:T(8,128)(2,1)} %all-gather.3.cloned.1.call-done) | copy-start | bytes 16515076
  58.3 2.8 copy-start.24
  62.9 12.9 %copy-start.4 = (bf16[5376,256]{1,0:T(8,128)(2,1)S(1)}, bf16[5376,256]{1,0:T(8,128)(2,1)}, u32[]{:S(2)}) copy-start(bf16[5376,256]{1,0:T(8,128)(2,1)} %param.15) | copy-start | bytes 8257540
  62.9 12.9 %copy-start.12 = (f32[5376]{0:T(1024)S(1)}, f32[5376]{0:T(1024)}, u32[]{:S(2)}) copy-start(f32[5376]{0:T(1024)} %param.12) | copy-start | bytes 64516
  62.9 12.9 %copy-start.25 = (f32[512]{0:T(512)S(1)}, f32[512]{0:T(512)}, u32[]{:S(2)}) copy-start(f32[512]{0:T(512)} %copy-done.24) | copy-start | bytes 6148
  65.3 22.0 %collective-permute-start.3 = (bf16[512,2,128]{2,0,1:T(8,128)(2,1)S(1)}, bf16[512,2,128]{2,0,1:T(8,128)(2,1)S(1)}, u32[]{:S(2)}, u32[]{:S(2)}) collective-permute-start(bf16[512,2,128]{2,0,1:T(8,128)(2,1)S(1)} %pad_maximum_fusion.2), channel_id=1, source_target_pairs={{0,32},{8,40},{16,48},{24,56},{32,64},{40,72},{48,80},{56,88},{64,... | collective-permute-start | bytes 786440 | tf_op jit(solution)/shard_map/ppermute | solution.py:17
  72.7 14.6 %collective-permute-start.2 = (bf16[512,2,128]{2,0,1:T(8,128)(2,1)S(1)}, bf16[512,2,128]{2,0,1:T(8,128)(2,1)S(1)}, u32[]{:S(2)}, u32[]{:S(2)}) collective-permute-start(bf16[512,2,128]{2,0,1:T(8,128)(2,1)S(1)} %pad_maximum_fusion.2), channel_id=1, source_target_pairs={{0,64},{8,72},{16,80},{24,88},{32,96},{40,104},{48,112},{56,120},{... | collective-permute-start | bytes 786440 | tf_op jit(solution)/shard_map/ppermute | solution.py:17
  81.0 17.2 %collective-permute-start.1 = (bf16[512,2,128]{0,2,1:T(8,128)(2,1)}, bf16[512,2,128]{0,2,1:T(8,128)(2,1)}, u32[]{:S(2)}, u32[]{:S(2)}) collective-permute-start(bf16[512,2,128]{0,2,1:T(8,128)(2,1)} %bitcast), channel_id=1, source_target_pairs={{0,32},{8,40},{16,48},{24,56},{32,64},{40,72},{48,80},{56,88},{64,... | collective-permute-start | bytes 786440 | tf_op jit(solution)/shard_map/ppermute | solution.py:17
  84.5 13.7 %collective-permute-start = (bf16[512,2,128]{0,2,1:T(8,128)(2,1)}, bf16[512,2,128]{0,2,1:T(8,128)(2,1)}, u32[]{:S(2)}, u32[]{:S(2)}) collective-permute-start(bf16[512,2,128]{0,2,1:T(8,128)(2,1)} %bitcast), channel_id=1, source_target_pairs={{0,64},{8,72},{16,80},{24,88},{32,96},{40,104},{48,112},{56,120},{... | collective-permute-start | bytes 786440 | tf_op jit(solution)/shard_map/ppermute | solution.py:17
  98.2 4.0 %copy-start.1 = (bf16[1536,2,128]{2,0,1:T(8,128)(2,1)}, bf16[1536,2,128]{2,0,1:T(8,128)(2,1)S(1)}, u32[]{:S(2)}) copy-start(bf16[1536,2,128]{2,0,1:T(8,128)(2,1)S(1)} %get-tuple-element.195) | copy-start | bytes 2359300
  126.8 1.2 copy-start.9
  126.8 1.2 copy-start.10
  126.8 1.2 copy-start.16
  126.8 1.2 copy-start.17
  126.8 1.2 copy-start.18
  126.8 3.8 %copy-start.13 = (f32[5376]{0:T(1024)S(1)}, f32[5376]{0:T(1024)}, u32[]{:S(2)}) copy-start(f32[5376]{0:T(1024)} %param.12) | copy-start | bytes 64516
  126.8 3.7 %copy-start.26 = (f32[512]{0:T(512)S(1)}, f32[512]{0:T(512)}, u32[]{:S(2)}) copy-start(f32[512]{0:T(512)} %copy-done.24) | copy-start | bytes 6148
  130.6 7.7 %copy-start.21 = (f32[128]{0:T(128)S(1)}, f32[128]{0:T(128)}, u32[]{:S(2)}) copy-start(f32[128]{0:T(128)} %param.16) | copy-start | bytes 1540
  130.6 7.9 %copy-start.6 = (f32[512,64]{0,1:T(8,128)S(1)}, f32[512,64]{0,1:T(8,128)}, u32[]{:S(2)}) copy-start(f32[512,64]{0,1:T(8,128)} %copy-done.5) | copy-start | bytes 393220
  130.6 7.9 %copy-start.8 = (f32[512,64]{0,1:T(8,128)S(1)}, f32[512,64]{0,1:T(8,128)}, u32[]{:S(2)}) copy-start(f32[512,64]{0,1:T(8,128)} %copy-done.7) | copy-start | bytes 393220
  138.3 5.1 %copy-start.2 = (bf16[1536,2,128]{2,0,1:T(8,128)(2,1)S(1)}, bf16[1536,2,128]{2,0,1:T(8,128)(2,1)}, u32[]{:S(2)}) copy-start(bf16[1536,2,128]{2,0,1:T(8,128)(2,1)} %copy-done.1) | copy-start | bytes 2359300
  153.0 138.0 %copy-start.22 = (pred[16,4]{0,1:T(4,128)(4,1)S(1)}, pred[16,4]{0,1:T(4,128)(4,1)}, u32[]{:S(2)}) copy-start(pred[16,4]{0,1:T(4,128)(4,1)} %iota_compare_fusion) | copy-start | bytes 196
  157.1 136.5 %copy-start.14 = (f32[16,2,1,2]{0,3,1,2:T(2,128)S(1)}, f32[16,2,1,2]{0,3,1,2:T(2,128)}, u32[]{:S(2)}) copy-start(f32[16,2,1,2]{0,3,1,2:T(2,128)} %copy.101) | copy-start | bytes 772
  157.1 136.8 %copy-start.15 = (f32[2,2,8,128]{3,2,0,1:T(8,128)S(1)}, f32[2,2,8,128]{3,2,0,1:T(8,128)}, u32[]{:S(2)}) copy-start(f32[2,2,8,128]{3,2,0,1:T(8,128)} %copy.121) | copy-start | bytes 49156
  290.9 3.0 %copy-start.28 = (bf16[4,1024,2,128]{3,1,0,2:T(8,128)(2,1)S(1)}, bf16[4,1024,2,128]{3,1,0,2:T(8,128)(2,1)}, u32[]{:S(2)}) copy-start(bf16[4,1024,2,128]{3,1,0,2:T(8,128)(2,1)} %get-tuple-element.74) | copy-start | bytes 6291460
  (4 other events, 3.9 us)
Sparse Core Ops, SparseCore 0:
  9.8 44.2 all-gather.2
  127.0 163.9 all-reduce.3
where the time goes:
time: 305 us; the launch traced here: 302 us
  waiting for transfers between devices  145 us (48%)
  local copies, waits for them, and re-layouts  43.3 us (14%)
  matrix products  38.7 us (13%)
  other arithmetic  27.1 us (9%)
  starting transfers between devices  16.8 us (6%)
  blocking collectives  16 us (5%)
  between operations  14.6 us (5%)
    psum x1, waiting for transfers between devices, local(): lax.psum(jnp.where(owner, local_values, zero_value), 'ctx')  133 us
    gather x32, local copies, waits for them, and re-layouts  29 us
    ppermute x4, starting transfers between devices, shifted(): lax.ppermute(value, axis, [(source, source + steps) for source in range(i...  16.8 us
    all_gather x1, blocking collectives, local(): lax.all_gather(decode_states, 'tp', axis=1, tiled=True)  16 us
    all_gather x1, waiting for transfers between devices, local(): lax.all_gather(prompt_states, 'tp', axis=1, tiled=True)  11.8 us
    dot_general x2, matrix products, advance(): jnp.dot(scaled, query_weight, preferred_element_type=jnp.float32)  11.1 us
    sub x1, matrix products, local(): weights = jnp.where(visible, jnp.exp(scores - row_top), 0.0)  9.54 us
    dot_general x2, matrix products, advance(): jnp.dot(scaled, value_weight, preferred_element_type=jnp.float32)  7.41 us
  transfers between devices with their start and end apart: 6, of which 2 were waited for; matrix products, arithmetic and copies ran while one was open for 21% of the time, Pallas kernels for 0%

commit v1 on v0

v1 whole, which is shorter than its diff:
```python
import functools
import math

import jax
import jax.numpy as jnp
import numpy as np
from jax import lax
from jax.experimental import pallas as pl
from jax.experimental.pallas import tpu as pltpu
from jax.sharding import PartitionSpec as P

MESH = pl.DeviceIdType.MESH
F32, BF16 = jnp.float32, jnp.bfloat16
WINDOW = 1024
PROMPTS = 4
EPS = 1e-06
SCORE_SCALE = 168.0 ** (-0.5)
HD = 128
NY, NZ, NX = 4, 8, 4
CH = 128
NCH = 4
NEG = -1e30


def dot(a, b, dims):
    return lax.dot_general(a, b, (dims, ((), ())), preferred_element_type=F32)


def kernel(
    feature_count,
    x_ref, xd_ref, gcol_ref, grow_ref, rp_ref, freq_ref, sgn_ref, qg_ref, kg_ref, len_ref,
    wq_hbm, wk_hbm, wv_hbm,
    out_ref, dout_ref,
    xg, xd, ss, wkv, wq, kv, relay, q_s, dqg, dk_s, dv_s, dpart, b1, p2, b2,
    ag_send, ag_recv, wsem, h_send, h_recv,
    dq1_send, dq1_recv, dq2_send, dq2_recv, r1_send, r1_recv, r2_send, r2_recv,
):
    me_c = lax.axis_index("ctx")
    me_t = lax.axis_index("tp")
    x, c = me_t // 2, lax.rem(me_t, 2)
    y, z = me_c // NZ, lax.rem(me_c, NZ)
    way = 1 - 2 * c
    feat = x_ref.shape[0]
    block = 2 * y + z // 4
    prompt = lax.rem(z, PROMPTS)

    def tp_of(xx, cc):
        return lax.rem(xx + NX, NX) * 2 + cc

    def ctx_of(yy, zz):
        return lax.rem(yy + NY, NY) * NZ + lax.rem(zz + NZ, NZ)

    near_a, near_b, far = tp_of(x - way, c), tp_of(x + way, c), tp_of(x + 2, c)
    partner = tp_of(x, 1 - c)
    from_partner = (partner, tp_of(x + way, 1 - c), tp_of(x - way, 1 - c), tp_of(x + 2, 1 - c))
    z_two, z_two_in = z + 2 * way, z - 2 * way
    source_z = lax.rem(z_two_in + NZ, NZ)
    out_b1 = ctx_of(y + source_z // 4, z_two)
    in_b1 = ctx_of(y - (1 - z // 4), z_two_in)

    weights = (
        pltpu.make_async_copy(wk_hbm, wkv.at[:, 0:256], wsem.at[0]),
        pltpu.make_async_copy(wv_hbm, wkv.at[:, 256:512], wsem.at[1]),
        pltpu.make_async_copy(wq_hbm, wq, wsem.at[2]),
    )
    for copy in weights:
        copy.start()

    barrier = pltpu.get_barrier_semaphore()
    for device in (
        [(me_c, t) for t in (near_a, near_b, partner)]
        + [(ctx_of(y, z + j), me_t) for j in range(1, NZ)]
        + [(ctx_of(y + j, z), me_t) for j in range(1, NY)]
        + [(in_b1, me_t)]
    ):
        pl.semaphore_signal(barrier, inc=1, device_id=device, device_id_type=MESH)

    decode_wide = xd_ref[...].astype(F32)
    xd[me_t] = (decode_wide * grow_ref[...]).astype(BF16)
    decode_sum = jnp.sum(decode_wide * decode_wide, axis=1, keepdims=True)
    ss[me_t, 4:6] = jnp.broadcast_to(decode_sum, (16, 128)).reshape(2, 8, 128)
    for k in range(NCH):
        wide = x_ref[:, k * CH : (k + 1) * CH].astype(F32)
        xg[k, me_t] = (wide * gcol_ref[...]).astype(BF16)
        ss[me_t, k] = jnp.sum((wide * wide).reshape(feat // 8, 8, CH), axis=0)

    pl.semaphore_wait(barrier, 14)

    def piece(k, d):
        if isinstance(k, int) and k == 4:
            return xd.at[d]
        if isinstance(k, int) and k == 5:
            return ss.at[d]
        return xg.at[k, d]

    def ag(k, d, j, target):
        return pltpu.make_async_remote_copy(
            src_ref=piece(k, d), dst_ref=piece(k, d),
            send_sem=ag_send.at[k, j], recv_sem=ag_recv.at[k, j],
            device_id=(me_c, target), device_id_type=MESH,
        )

    def start_own(k):
        ag(k, me_t, 0, near_b).start()
        ag(k, me_t, 1, near_a).start()
        ag(k, me_t, 3, partner).start()

    def phase_a(k):
        ag(k, near_a, 0, near_b).wait_recv()
        ag(k, near_a, 2, near_b).start()
        ag(k, near_a, 4, partner).start()

    def phase_b(k):
        ag(k, near_b, 1, near_b).wait_recv()
        ag(k, near_b, 5, partner).start()

    def phase_c(k):
        ag(k, far, 2, near_b).wait_recv()
        ag(k, far, 6, partner).start()
        for j in range(4):
            ag(k, from_partner[j], 3 + j, near_b).wait_recv()

    def ag_sent(k):
        for j in range(7):
            ag(k, me_t, j, near_b).wait_send()

    def halo(kind, s):
        src, dst, target = (
            (kv.at[8 + s], kv.at[s], ctx_of(y + 1, z)),
            (kv.at[8 + s], relay.at[s], ctx_of(y, z_two)),
            (relay.at[s], kv.at[4 + s], out_b1),
        )[kind]
        return pltpu.make_async_remote_copy(
            src_ref=src, dst_ref=dst, send_sem=h_send.at[kind, s], recv_sem=h_recv.at[kind, s],
            device_id=(target, me_t), device_id_type=MESH,
        )

    def pass_on(s):
        halo(1, s).wait_recv()
        halo(2, s).start()

    freq, sgn = freq_ref[...], sgn_ref[...]

    def rope_tables(positions):
        angles = positions * freq
        return jnp.cos(angles), jnp.sin(angles) * sgn

    def head(acc, gain, tables):
        unit = acc * lax.rsqrt(jnp.mean(acc * acc, axis=1, keepdims=True) + EPS) * gain
        return (unit * tables[0] + pltpu.roll(unit, HD // 2, axis=1) * tables[1]).astype(BF16)

    qg, kg = qg_ref[...], kg_ref[...]

    start_own(5)
    start_own(4)
    start_own(0)
    start_own(1)
    for k in (5, 4):
        phase_a(k)
        phase_b(k)
    for k in (5, 4):
        phase_c(k)

    for copy in weights:
        copy.wait()
    acc_kv = jnp.zeros((16, 512), F32)
    acc_q = jnp.zeros((16, 512), F32)
    for d in range(8):
        rows = slice(d * feat, (d + 1) * feat)
        acc_kv += dot(xd[d], wkv[rows, :], ((1,), (0,)))
        acc_q += dot(xd[d], wq[rows, :], ((1,), (0,)))
    rp = rp_ref[...]
    decode_pos = jnp.zeros((16, 128), jnp.int32)
    for p in range(PROMPTS):
        decode_pos = jnp.where(rp == p, len_ref[p], decode_pos)
    tables = rope_tables(decode_pos.astype(F32))
    sums = jnp.sum(ss[:, 4:6], axis=0).reshape(16, 128)
    inverse = lax.rsqrt(sums / feature_count + EPS)
    for h in range(4):
        dqg[me_c, :, h * HD : (h + 1) * HD] = head(
            acc_q[:, h * HD : (h + 1) * HD] * inverse, qg, tables
        )
    for h in range(2):
        dk_s[:, h * HD : (h + 1) * HD] = head(
            acc_kv[:, h * HD : (h + 1) * HD] * inverse, kg, tables
        )
        dv_s[:, h * HD : (h + 1) * HD] = (
            acc_kv[:, 256 + h * HD : 256 + (h + 1) * HD] * inverse
        ).astype(BF16)

    def dq1(j, owner_z, target_z):
        slot = dqg.at[ctx_of(y, owner_z)]
        return pltpu.make_async_remote_copy(
            src_ref=slot, dst_ref=slot, send_sem=dq1_send.at[j - 1], recv_sem=dq1_recv.at[j - 1],
            device_id=(ctx_of(y, target_z), me_t), device_id_type=MESH,
        )

    def dq2(j, owner_y, target_y):
        slots = dqg.at[pl.ds(lax.rem(owner_y + NY, NY) * NZ, NZ)]
        return pltpu.make_async_remote_copy(
            src_ref=slots, dst_ref=slots, send_sem=dq2_send.at[j - 1], recv_sem=dq2_recv.at[j - 1],
            device_id=(ctx_of(target_y, z), me_t), device_id_type=MESH,
        )

    for j in range(1, NZ):
        dq1(j, z, z + j).start()

    row_index = lax.broadcasted_iota(jnp.int32, (CH, 1), 0)
    phase_a(0)
    start_own(2)
    phase_b(0)

    def project(s, carry):
        @pl.when(s < NCH - 1)
        def _():
            phase_a(s + 1)

        @pl.when(s < NCH - 3)
        def _():
            start_own(s + 3)

        @pl.when(s < NCH - 1)
        def _():
            phase_b(s + 1)

        phase_c(s)
        states = xg[s].reshape(8 * feat, CH)
        sums = jnp.sum(jnp.transpose(jnp.sum(ss[:, s], axis=0)), axis=1, keepdims=True)
        inverse = lax.rsqrt(sums / feature_count + EPS)
        tables = rope_tables((block * 512 + s * CH + row_index).astype(F32))
        acc = dot(states, wkv[...], ((0,), (0,)))
        for h in range(2):
            kv[8 + s, :, h * HD : (h + 1) * HD] = head(
                acc[:, h * HD : (h + 1) * HD] * inverse, kg, tables
            )
        kv[8 + s, :, 256:512] = (acc[:, 256:512] * inverse).astype(BF16)
        halo(0, s).start()
        halo(1, s).start()
        acc = dot(states, wq[...], ((0,), (0,)))
        for h in range(4):
            q_s[s, :, h * HD : (h + 1) * HD] = head(
                acc[:, h * HD : (h + 1) * HD] * inverse, qg, tables
            )

        @pl.when(s > 0)
        def _():
            pass_on(s - 1)

        @pl.when(s == 0)
        def _():
            for j in range(1, NZ):
                dq1(j, z - j, z).wait_recv()
            for j in range(1, NY):
                dq2(j, y, y + j).start()

        return carry

    lax.fori_loop(0, NCH, project, 0)
    pass_on(NCH - 1)

    for j in range(1, NY):
        dq2(j, y - j, y).wait_recv()
    length = len_ref[prompt]
    key_pos = block * 512 + lax.broadcasted_iota(jnp.int32, (1, 512), 1)
    bias = jnp.where((key_pos >= length - WINDOW) & (key_pos < length), 0.0, NEG)
    lane = lax.broadcasted_iota(jnp.int32, (1, 128), 1)

    def pack(lse_list):
        packed = None
        for h, lse in enumerate(lse_list):
            high = lse.astype(BF16).astype(F32)
            middle = (lse - high).astype(BF16).astype(F32)
            low = lse - high - middle
            term = (
                jnp.where(lane == h, high, 0.0)
                + jnp.where(lane == 4 + h, middle, 0.0)
                + jnp.where(lane == 8 + h, low, 0.0)
            )
            packed = term if packed is None else packed + term
        return packed.astype(BF16)

    def lse_of(packed, h):
        wide = packed.astype(F32)
        return wide[:, h : h + 1] + wide[:, 4 + h : 5 + h] + wide[:, 8 + h : 9 + h]

    queries = dqg[...].reshape(512, 512)
    keys = kv[8:12].reshape(512, 512)
    lse_list = []
    for h in range(4):
        g = h // 2
        scores = dot(
            queries[:, h * HD : (h + 1) * HD], keys[:, g * HD : (g + 1) * HD], ((1,), (1,))
        )
        scores = scores * SCORE_SCALE + bias
        top = jnp.max(scores, axis=1, keepdims=True)
        weights_h = jnp.exp(scores - top)
        total = jnp.sum(weights_h, axis=1, keepdims=True)
        mixed = dot(
            weights_h.astype(BF16), keys[:, 256 + g * HD : 256 + (g + 1) * HD], ((1,), (0,))
        )
        dpart[:, :, h * HD : (h + 1) * HD] = (mixed / total).astype(BF16).reshape(32, 16, HD)
        lse_list.append(top + jnp.log(total))
    dpart[:, :, 512:640] = pack(lse_list).reshape(32, 16, 128)

    def r1(j, slot_y, target_y):
        return pltpu.make_async_remote_copy(
            src_ref=dpart.at[pl.ds(lax.rem(target_y + NY, NY) * NZ, NZ)],
            dst_ref=b1.at[lax.rem(slot_y + NY, NY)],
            send_sem=r1_send.at[j - 1], recv_sem=r1_recv.at[j - 1],
            device_id=(ctx_of(target_y, z), me_t), device_id_type=MESH,
        )

    def r2(j, slot_z, target_z):
        return pltpu.make_async_remote_copy(
            src_ref=p2.at[lax.rem(target_z + NZ, NZ)],
            dst_ref=b2.at[lax.rem(slot_z + NZ, NZ)],
            send_sem=r2_send.at[j - 1], recv_sem=r2_recv.at[j - 1],
            device_id=(ctx_of(y, target_z), me_t), device_id_type=MESH,
        )

    for j in range(1, NY):
        r1(j, y, y + j).start()
    b1[y] = dpart[pl.ds(y * NZ, NZ)]

    for s in range(NCH):
        halo(0, s).wait_recv()
        halo(2, s).wait_recv()
    width = WINDOW + CH
    rows2 = lax.rem(lax.broadcasted_iota(jnp.int32, (2 * CH, 1), 0), CH)
    cols = lax.broadcasted_iota(jnp.int32, (1, CH), 1)
    columns = lax.broadcasted_iota(jnp.int32, (1, width), 1)

    def attend(i, carry):
        low = jnp.where(columns >= (2 - block) * 512 - i * CH, 0.0, NEG)
        alive = block * 512 + i * CH + rows2 < length
        for g in range(2):
            query = jnp.concatenate(
                [q_s[i, :, (2 * g + r) * HD : (2 * g + r + 1) * HD] for r in range(2)], axis=0
            )
            window = kv[pl.ds(i, 9)].reshape(width, 512)
            scores = dot(query, window[:, g * HD : (g + 1) * HD], ((1,), (1,)))
            scores = scores * SCORE_SCALE + low
            scores = jnp.concatenate(
                [
                    jnp.where(cols > rows2, scores[:, :CH], NEG),
                    scores[:, CH:WINDOW],
                    jnp.where(cols <= rows2, scores[:, WINDOW:], NEG),
                ],
                axis=1,
            )
            top = jnp.max(scores, axis=1, keepdims=True)
            weights_h = jnp.exp(scores - top)
            total = jnp.sum(weights_h, axis=1, keepdims=True)
            mixed = dot(
                weights_h.astype(BF16),
                window[:, 256 + g * HD : 256 + (g + 1) * HD],
                ((1,), (0,)),
            )
            mixed = jnp.where(alive, mixed / total, 0.0).astype(BF16)
            for r in range(2):
                out_ref[
                    pl.ds(pl.multiple_of(i * CH, CH), CH),
                    (2 * g + r) * HD : (2 * g + r + 1) * HD,
                ] = mixed[r * CH : (r + 1) * CH]
        return carry

    lax.fori_loop(0, NCH, attend, 0)

    for j in range(1, NY):
        r1(j, y - j, y).wait_recv()

    def merge(parts, masks, h):
        lses = [lse_of(part[:, 512:640], h) for part in parts]
        if masks is not None:
            lses = [jnp.where(mask, lse, NEG) for mask, lse in zip(masks, lses)]
        top = functools.reduce(jnp.maximum, lses)
        factors = [jnp.exp(lse - top) for lse in lses]
        total = sum(factors)
        mixed = sum(
            f * part[:, h * HD : (h + 1) * HD].astype(F32) for f, part in zip(factors, parts)
        )
        return top, total, mixed

    parts = [b1[i].reshape(128, 640) for i in range(NY)]
    lse_list = []
    for h in range(4):
        top, total, mixed = merge(parts, None, h)
        p2[:, :, h * HD : (h + 1) * HD] = (mixed / total).astype(BF16).reshape(8, 16, HD)
        lse_list.append(top + jnp.log(total))
    p2[:, :, 512:640] = pack(lse_list).reshape(8, 16, 128)
    for j in range(1, NZ):
        r2(j, z, z + j).start()
    b2[z] = p2[z]
    for j in range(1, NZ):
        r2(j, z - j, z).wait_recv()
    parts = [b2[i] for i in range(NZ)]
    masks = [rp[:, :1] == i % PROMPTS for i in range(NZ)]
    own_query = dqg[me_c].astype(F32)
    for h in range(4):
        g = h // 2
        top, total, mixed = merge(parts, masks, h)
        own = (
            jnp.sum(
                own_query[:, h * HD : (h + 1) * HD]
                * dk_s[:, g * HD : (g + 1) * HD].astype(F32),
                axis=1,
                keepdims=True,
            )
            * SCORE_SCALE
        )
        new_top = jnp.maximum(top, own)
        shift = jnp.exp(top - new_top)
        weight = jnp.exp(own - new_top)
        value = dv_s[:, g * HD : (g + 1) * HD].astype(F32)
        dout_ref[:, h * HD : (h + 1) * HD] = (
            (mixed * shift + weight * value) / (total * shift + weight)
        ).astype(BF16)

    for k in range(6):
        ag_sent(k)
    for s in range(NCH):
        for kind in range(3):
            halo(kind, s).wait_send()
    for j in range(1, NZ):
        dq1(j, z, z + j).wait_send()
        r2(j, z, z + j).wait_send()
    for j in range(1, NY):
        dq2(j, y, y + j).wait_send()
        r1(j, y, y + j).wait_send()


def local(
    prompt_states,
    decode_states,
    norm_gain,
    query_weight,
    key_weight,
    value_weight,
    query_gain,
    key_gain,
    prompt_lengths,
    row_prompt,
):
    tok_rows, feat = prompt_states.shape
    dec_rows = decode_states.shape[0]
    feature_count = norm_gain.shape[0]
    half = HD // 2
    mine = lax.dynamic_slice(norm_gain, (lax.axis_index("tp") * feat,), (feat,))
    gain_column = jnp.broadcast_to(mine[:, None], (feat, 128))
    frequency = np.array([10000.0 ** (-2.0 * (j % half) / HD) for j in range(HD)], np.float32)
    sign = np.array([-1.0] * half + [1.0] * half, np.float32)
    rows = jnp.broadcast_to(row_prompt[:, None], (dec_rows, 128))
    vmem = pl.BlockSpec(memory_space=pltpu.VMEM)
    hbm = pl.BlockSpec(memory_space=pl.ANY)
    dma = pltpu.SemaphoreType.DMA
    return pl.pallas_call(
        functools.partial(kernel, float(feature_count)),
        out_shape=(
            jax.ShapeDtypeStruct((tok_rows, 512), BF16),
            jax.ShapeDtypeStruct((dec_rows, 512), BF16),
        ),
        in_specs=[vmem] * 9 + [pl.BlockSpec(memory_space=pltpu.SMEM)] + [hbm] * 3,
        out_specs=(vmem, vmem),
        scratch_shapes=[
            pltpu.VMEM((NCH, 8, feat, CH), BF16),
            pltpu.VMEM((8, dec_rows, feat), BF16),
            pltpu.VMEM((8, 6, 8, 128), F32),
            pltpu.VMEM((feature_count, 512), BF16),
            pltpu.VMEM((feature_count, 512), BF16),
            pltpu.VMEM((12, CH, 512), BF16),
            pltpu.VMEM((NCH, CH, 512), BF16),
            pltpu.VMEM((NCH, CH, 512), BF16),
            pltpu.VMEM((32, dec_rows, 512), BF16),
            pltpu.VMEM((dec_rows, 256), BF16),
            pltpu.VMEM((dec_rows, 256), BF16),
            pltpu.VMEM((32, dec_rows, 640), BF16),
            pltpu.VMEM((NY, NZ, dec_rows, 640), BF16),
            pltpu.VMEM((NZ, dec_rows, 640), BF16),
            pltpu.VMEM((NZ, dec_rows, 640), BF16),
            dma((6, 7)), dma((6, 7)), dma((3,)), dma((3, NCH)), dma((3, NCH)),
            dma((NZ - 1,)), dma((NZ - 1,)), dma((NY - 1,)), dma((NY - 1,)),
            dma((NY - 1,)), dma((NY - 1,)), dma((NZ - 1,)), dma((NZ - 1,)),
        ],
        compiler_params=pltpu.CompilerParams(
            collective_id=0, has_side_effects=True, vmem_limit_bytes=60 * 2**20
        ),
    )(
        prompt_states.T,
        decode_states,
        gain_column,
        mine[None, :],
        rows,
        jnp.asarray(frequency)[None, :],
        jnp.asarray(sign)[None, :],
        query_gain[None, :],
        key_gain[None, :],
        prompt_lengths,
        query_weight,
        key_weight,
        value_weight,
    )


def solution(mesh):
    placed = (
        P("ctx", "tp"),
        P("ctx", "tp"),
        P(),
        P(None, "tp"),
        P(None, "tp"),
        P(None, "tp"),
        P(),
        P(),
        P(),
        P("ctx"),
    )
    return jax.shard_map(
        local,
        mesh=mesh,
        in_specs=placed,
        out_specs=(P("ctx", "tp"), P("ctx", "tp")),
        check_vma=False,
    )
```

time: 305 us -> 88.5 us (0.29)
  waiting for transfers between devices: 145 us -> 0 us
  Pallas kernels: 0 us -> 80.8 us
  matrix products: 38.7 us -> 0 us
  local copies, waits for them, and re-layouts: 43.3 us -> 6.77 us
  other arithmetic: 27.1 us -> 0 us
  starting transfers between devices: 16.8 us -> 0 us
  blocking collectives: 16 us -> 0 us
  between operations: 14.6 us -> 0.64 us
    psum x1 -> x0, waiting for transfers between devices: 133 us -> none  [local(): lax.psum(jnp.where(owner, local_values, zero_value), 'ctx')]
    pallas_call x0 -> x1, Pallas kernels: none -> 80.8 us  [local(): pl.pallas_call(functools.partial(kernel, float(feature_count)), out_shape...]
    dot_general x10 -> x0, matrix products: 29.1 us -> none  [the longest x2 11.1 us: advance(): jnp.dot(scaled, query_weight, preferred_element_type=jnp.float32)]
    gather x32 -> x0, local copies, waits for them, and re-layouts: 29 us -> none
    ppermute x4 -> x0, starting transfers between devices: 16.8 us -> none  [shifted(): lax.ppermute(value, axis, [(source, source + steps) for source in range(i...]
    all_gather x1 -> x0, blocking collectives: 16 us -> none  [local(): lax.all_gather(decode_states, 'tp', axis=1, tiled=True)]
    all_gather x1 -> x0, waiting for transfers between devices: 11.8 us -> none  [local(): lax.all_gather(prompt_states, 'tp', axis=1, tiled=True)]
    sub x1 -> x0, matrix products: 9.54 us -> none  [local(): weights = jnp.where(visible, jnp.exp(scores - row_top), 0.0)]
  transfers between devices with their start and end apart: 6 -> 0, of which waited for: 2 -> 0; matrix products, arithmetic and copies ran while one was open for 21% -> 0% of each run, Pallas kernels for 0% -> 0%
where the time goes in v1:
time: 88.5 us; the launch traced here: 88.2 us
  Pallas kernels  80.8 us (91%)
  local copies, waits for them, and re-layouts  6.77 us (8%)
    pallas_call x1, Pallas kernels, local(): pl.pallas_call(functools.partial(kernel, float(feature_count)), out_shape...  80.8 us
    unnamed x2, local copies, waits for them, and re-layouts  3.19 us

profile of v1, /device:TPU:1, one launch (start us, length us, event | category | flops | bytes accessed | tf_op | source)
XLA Modules:
  0.0 88.2 jit_solution(9095562997111795104)
XLA Ops:
  0.6 0.8 dynamic_slice.3
  1.4 0.6 broadcast_in_dim.28.grow_ref
  2.0 1.3 %broadcast_in_dim.29.rp_ref = s32[16,128]{1,0:T(8,128)} broadcast(s32[16]{0:T(128)} %param.21), dimensions={0} | broadcast | bytes 8256 | tf_op jit(solution)/shard_map/broadcast_in_dim | solution.py:452
  3.3 0.9 %broadcast_in_dim.27.gcol_ref = f32[672,128]{1,0:T(8,128)} broadcast(f32[672]{0:T(1024)S(1)} %dynamic_slice.3), dimensions={0} | broadcast | bytes 346752 | tf_op jit(solution)/shard_map/broadcast_in_dim | solution.py:449
  4.2 80.8 %shard_map.131 = (bf16[512,512]{1,0:T(8,128)(2,1)}, bf16[16,512]{1,0:T(8,128)(2,1)}) custom-call(bf16[672,512]{1,0:T(8,128)(2,1)} %bitcast.3, bf16[16,672]{1,0:T(8,128)(2,1)} %xd_ref.1, f32[672,128]{1,0:T(8,128)} %broadcast_in_dim.27.gcol_ref, f32[1,672]{1,0:T(1,128)} %broadcast_in_dim.28.grow_ref, s32[16,128]{1,0:T(8,128)} %broadcast_in_dim.29.rp_ref, ...), custom_call_target="tpu_custom_call" | custom-call | tf_op jit(solution)/shard_map/pallas_call | solution.py:456
  85.0 1.9 %copy.16 = bf16[512,512]{1,0:T(8,128)(2,1)} copy(bf16[512,512]{1,0:T(8,128)(2,1)} %get-tuple-element.4) | data formatting | bytes 1048576
  86.9 1.3 %copy.17 = bf16[16,512]{1,0:T(8,128)(2,1)} copy(bf16[16,512]{1,0:T(8,128)(2,1)} %get-tuple-element.5) | data formatting | bytes 32768

commit v2 on v1

--- a/solution.py
+++ b/solution.py
@@ -28,10 +28,10 @@
 
 def kernel(
     feature_count,
-    x_ref, xd_ref, gcol_ref, grow_ref, rp_ref, freq_ref, sgn_ref, qg_ref, kg_ref, len_ref,
+    x_ref, xd_ref, gain_ref, freq_ref, sgn_ref, qg_ref, kg_ref, len_ref, rp_ref,
     wq_hbm, wk_hbm, wv_hbm,
     out_ref, dout_ref,
-    xg, xd, ss, wkv, wq, kv, relay, q_s, dqg, dk_s, dv_s, dpart, b1, p2, b2,
+    xg, xd, ss, wkv, wq, kv, q_s, dqg, dk_s, dv_s, dpart, b1, p2, b2, top_s, sum_s, mix_s,
     ag_send, ag_recv, wsem, h_send, h_recv,
     dq1_send, dq1_recv, dq2_send, dq2_recv, r1_send, r1_recv, r2_send, r2_recv,
 ):
@@ -53,10 +53,8 @@
     near_a, near_b, far = tp_of(x - way, c), tp_of(x + way, c), tp_of(x + 2, c)
     partner = tp_of(x, 1 - c)
     from_partner = (partner, tp_of(x + way, 1 - c), tp_of(x - way, 1 - c), tp_of(x + 2, 1 - c))
-    z_two, z_two_in = z + 2 * way, z - 2 * way
-    source_z = lax.rem(z_two_in + NZ, NZ)
-    out_b1 = ctx_of(y + source_z // 4, z_two)
-    in_b1 = ctx_of(y - (1 - z // 4), z_two_in)
+    out_b1 = ctx_of(y + z // 4, z + 4)
+    in_b1 = ctx_of(y - (1 - z // 4), z + 4)
 
     weights = (
         pltpu.make_async_copy(wk_hbm, wkv.at[:, 0:256], wsem.at[0]),
@@ -68,23 +66,27 @@
 
     barrier = pltpu.get_barrier_semaphore()
     for device in (
-        [(me_c, t) for t in (near_a, near_b, partner)]
+        [(me_c, t) for t in (near_a, near_b, far, partner)]
         + [(ctx_of(y, z + j), me_t) for j in range(1, NZ)]
         + [(ctx_of(y + j, z), me_t) for j in range(1, NY)]
         + [(in_b1, me_t)]
     ):
         pl.semaphore_signal(barrier, inc=1, device_id=device, device_id_type=MESH)
 
+    gain_row = gain_ref[:, 0:feat]
+    for t in range(1, 8):
+        gain_row = jnp.where(me_t == t, gain_ref[:, t * feat : (t + 1) * feat], gain_row)
+    gain_column = jnp.transpose(jnp.broadcast_to(gain_row, (128, feat)))
     decode_wide = xd_ref[...].astype(F32)
-    xd[me_t] = (decode_wide * grow_ref[...]).astype(BF16)
+    xd[me_t] = (decode_wide * gain_row).astype(BF16)
     decode_sum = jnp.sum(decode_wide * decode_wide, axis=1, keepdims=True)
     ss[me_t, 4:6] = jnp.broadcast_to(decode_sum, (16, 128)).reshape(2, 8, 128)
     for k in range(NCH):
         wide = x_ref[:, k * CH : (k + 1) * CH].astype(F32)
-        xg[k, me_t] = (wide * gcol_ref[...]).astype(BF16)
+        xg[k, me_t] = (wide * gain_column).astype(BF16)
         ss[me_t, k] = jnp.sum((wide * wide).reshape(feat // 8, 8, CH), axis=0)
 
-    pl.semaphore_wait(barrier, 14)
+    pl.semaphore_wait(barrier, 15)
 
     def piece(k, d):
         if isinstance(k, int) and k == 4:
@@ -103,20 +105,13 @@
     def start_own(k):
         ag(k, me_t, 0, near_b).start()
         ag(k, me_t, 1, near_a).start()
+        ag(k, me_t, 2, far).start()
         ag(k, me_t, 3, partner).start()
 
-    def phase_a(k):
-        ag(k, near_a, 0, near_b).wait_recv()
-        ag(k, near_a, 2, near_b).start()
-        ag(k, near_a, 4, partner).start()
-
-    def phase_b(k):
-        ag(k, near_b, 1, near_b).wait_recv()
-        ag(k, near_b, 5, partner).start()
-
-    def phase_c(k):
-        ag(k, far, 2, near_b).wait_recv()
-        ag(k, far, 6, partner).start()
+    def gather(k):
+        for j, d in enumerate((near_a, near_b, far)):
+            ag(k, d, j, near_b).wait_recv()
+            ag(k, d, 4 + j, partner).start()
         for j in range(4):
             ag(k, from_partner[j], 3 + j, near_b).wait_recv()
 
@@ -125,19 +120,12 @@
             ag(k, me_t, j, near_b).wait_send()
 
     def halo(kind, s):
-        src, dst, target = (
-            (kv.at[8 + s], kv.at[s], ctx_of(y + 1, z)),
-            (kv.at[8 + s], relay.at[s], ctx_of(y, z_two)),
-            (relay.at[s], kv.at[4 + s], out_b1),
-        )[kind]
+        slot, target = ((4 + s, ctx_of(y + 1, z)), (s, out_b1))[kind]
         return pltpu.make_async_remote_copy(
-            src_ref=src, dst_ref=dst, send_sem=h_send.at[kind, s], recv_sem=h_recv.at[kind, s],
+            src_ref=kv.at[8 + s], dst_ref=kv.at[slot],
+            send_sem=h_send.at[kind, s], recv_sem=h_recv.at[kind, s],
             device_id=(target, me_t), device_id_type=MESH,
         )
-
-    def pass_on(s):
-        halo(1, s).wait_recv()
-        halo(2, s).start()
 
     freq, sgn = freq_ref[...], sgn_ref[...]
 
@@ -151,15 +139,10 @@
 
     qg, kg = qg_ref[...], kg_ref[...]
 
-    start_own(5)
-    start_own(4)
-    start_own(0)
-    start_own(1)
+    for k in (5, 4, 0, 1, 2, 3):
+        start_own(k)
     for k in (5, 4):
-        phase_a(k)
-        phase_b(k)
-    for k in (5, 4):
-        phase_c(k)
+        gather(k)
 
     for copy in weights:
         copy.wait()
@@ -169,7 +152,10 @@
         rows = slice(d * feat, (d + 1) * feat)
         acc_kv += dot(xd[d], wkv[rows, :], ((1,), (0,)))
         acc_q += dot(xd[d], wq[rows, :], ((1,), (0,)))
-    rp = rp_ref[...]
+    rows16 = lax.broadcasted_iota(jnp.int32, (16, 128), 0)
+    rp = jnp.zeros((16, 128), jnp.int32)
+    for r in range(16):
+        rp = jnp.where(rows16 == r, rp_ref[r], rp)
     decode_pos = jnp.zeros((16, 128), jnp.int32)
     for p in range(PROMPTS):
         decode_pos = jnp.where(rp == p, len_ref[p], decode_pos)
@@ -206,24 +192,9 @@
         dq1(j, z, z + j).start()
 
     row_index = lax.broadcasted_iota(jnp.int32, (CH, 1), 0)
-    phase_a(0)
-    start_own(2)
-    phase_b(0)
 
     def project(s, carry):
-        @pl.when(s < NCH - 1)
-        def _():
-            phase_a(s + 1)
-
-        @pl.when(s < NCH - 3)
-        def _():
-            start_own(s + 3)
-
-        @pl.when(s < NCH - 1)
-        def _():
-            phase_b(s + 1)
-
-        phase_c(s)
+        gather(s)
         states = xg[s].reshape(8 * feat, CH)
         sums = jnp.sum(jnp.transpose(jnp.sum(ss[:, s], axis=0)), axis=1, keepdims=True)
         inverse = lax.rsqrt(sums / feature_count + EPS)
@@ -242,11 +213,7 @@
                 acc[:, h * HD : (h + 1) * HD] * inverse, qg, tables
             )
 
-        @pl.when(s > 0)
-        def _():
-            pass_on(s - 1)
-
-        @pl.when(s == 0)
+        @pl.when(s == 1)
         def _():
             for j in range(1, NZ):
                 dq1(j, z - j, z).wait_recv()
@@ -256,7 +223,6 @@
         return carry
 
     lax.fori_loop(0, NCH, project, 0)
-    pass_on(NCH - 1)
 
     for j in range(1, NY):
         dq2(j, y - j, y).wait_recv()
@@ -322,41 +288,59 @@
         r1(j, y, y + j).start()
     b1[y] = dpart[pl.ds(y * NZ, NZ)]
 
+    def query_of(i, g):
+        return jnp.concatenate(
+            [q_s[i, :, (2 * g + r) * HD : (2 * g + r + 1) * HD] for r in range(2)], axis=0
+        )
+
+    def softmax(scores, window, g):
+        top = jnp.max(scores, axis=1, keepdims=True)
+        weights_h = jnp.exp(scores - top)
+        total = jnp.sum(weights_h, axis=1, keepdims=True)
+        values = window[:, 256 + g * HD : 256 + (g + 1) * HD]
+        return top, total, dot(weights_h.astype(BF16), values, ((1,), (0,)))
+
     for s in range(NCH):
         halo(0, s).wait_recv()
-        halo(2, s).wait_recv()
-    width = WINDOW + CH
+    width = 5 * CH
     rows2 = lax.rem(lax.broadcasted_iota(jnp.int32, (2 * CH, 1), 0), CH)
     cols = lax.broadcasted_iota(jnp.int32, (1, CH), 1)
     columns = lax.broadcasted_iota(jnp.int32, (1, width), 1)
 
-    def attend(i, carry):
-        low = jnp.where(columns >= (2 - block) * 512 - i * CH, 0.0, NEG)
-        alive = block * 512 + i * CH + rows2 < length
+    def attend_first(i, carry):
+        low = jnp.where((block >= 2) | (columns >= (4 - i) * CH), 0.0, NEG)
         for g in range(2):
-            query = jnp.concatenate(
-                [q_s[i, :, (2 * g + r) * HD : (2 * g + r + 1) * HD] for r in range(2)], axis=0
-            )
-            window = kv[pl.ds(i, 9)].reshape(width, 512)
-            scores = dot(query, window[:, g * HD : (g + 1) * HD], ((1,), (1,)))
+            window = kv[pl.ds(4 + i, 5)].reshape(width, 512)
+            scores = dot(query_of(i, g), window[:, g * HD : (g + 1) * HD], ((1,), (1,)))
             scores = scores * SCORE_SCALE + low
             scores = jnp.concatenate(
                 [
                     jnp.where(cols > rows2, scores[:, :CH], NEG),
-                    scores[:, CH:WINDOW],
-                    jnp.where(cols <= rows2, scores[:, WINDOW:], NEG),
+                    scores[:, CH : 4 * CH],
+                    jnp.where(cols <= rows2, scores[:, 4 * CH :], NEG),
                 ],
                 axis=1,
             )
-            top = jnp.max(scores, axis=1, keepdims=True)
-            weights_h = jnp.exp(scores - top)
-            total = jnp.sum(weights_h, axis=1, keepdims=True)
-            mixed = dot(
-                weights_h.astype(BF16),
-                window[:, 256 + g * HD : 256 + (g + 1) * HD],
-                ((1,), (0,)),
-            )
-            mixed = jnp.where(alive, mixed / total, 0.0).astype(BF16)
+            top, total, mixed = softmax(scores, window, g)
+            top_s[i, g], sum_s[i, g], mix_s[i, g] = top, total, mixed
+        return carry
+
+    lax.fori_loop(0, NCH, attend_first, 0)
+    for s in range(NCH):
+        halo(1, s).wait_recv()
+    absent = jnp.where(block == 0, NEG, 0.0)
+
+    def attend_last(i, carry):
+        alive = block * 512 + i * CH + rows2 < length
+        for g in range(2):
+            window = kv[0:4].reshape(512, 512)
+            scores = dot(query_of(i, g), window[:, g * HD : (g + 1) * HD], ((1,), (1,)))
+            top, total, mixed = softmax(scores * SCORE_SCALE + absent, window, g)
+            first_top = top_s[i, g]
+            both = jnp.maximum(top, first_top)
+            f1, f2 = jnp.exp(first_top - both), jnp.exp(top - both)
+            mixed = (mix_s[i, g] * f1 + mixed * f2) / (sum_s[i, g] * f1 + total * f2)
+            mixed = jnp.where(alive, mixed, 0.0).astype(BF16)
             for r in range(2):
                 out_ref[
                     pl.ds(pl.multiple_of(i * CH, CH), CH),
@@ -364,7 +348,7 @@
                 ] = mixed[r * CH : (r + 1) * CH]
         return carry
 
-    lax.fori_loop(0, NCH, attend, 0)
+    lax.fori_loop(0, NCH, attend_last, 0)
 
     for j in range(1, NY):
         r1(j, y - j, y).wait_recv()
@@ -419,7 +403,7 @@
     for k in range(6):
         ag_sent(k)
     for s in range(NCH):
-        for kind in range(3):
+        for kind in range(2):
             halo(kind, s).wait_send()
     for j in range(1, NZ):
         dq1(j, z, z + j).wait_send()
@@ -427,6 +411,11 @@
     for j in range(1, NY):
         dq2(j, y, y + j).wait_send()
         r1(j, y, y + j).wait_send()
+
+
+def hand_over(a_ref, b_ref, a_out, b_out):
+    a_out[...] = a_ref[...]
+    b_out[...] = b_ref[...]
 
 
 def local(
@@ -445,21 +434,18 @@
     dec_rows = decode_states.shape[0]
     feature_count = norm_gain.shape[0]
     half = HD // 2
-    mine = lax.dynamic_slice(norm_gain, (lax.axis_index("tp") * feat,), (feat,))
-    gain_column = jnp.broadcast_to(mine[:, None], (feat, 128))
     frequency = np.array([10000.0 ** (-2.0 * (j % half) / HD) for j in range(HD)], np.float32)
     sign = np.array([-1.0] * half + [1.0] * half, np.float32)
-    rows = jnp.broadcast_to(row_prompt[:, None], (dec_rows, 128))
     vmem = pl.BlockSpec(memory_space=pltpu.VMEM)
     hbm = pl.BlockSpec(memory_space=pl.ANY)
     dma = pltpu.SemaphoreType.DMA
-    return pl.pallas_call(
+    attended = pl.pallas_call(
         functools.partial(kernel, float(feature_count)),
         out_shape=(
             jax.ShapeDtypeStruct((tok_rows, 512), BF16),
             jax.ShapeDtypeStruct((dec_rows, 512), BF16),
         ),
-        in_specs=[vmem] * 9 + [pl.BlockSpec(memory_space=pltpu.SMEM)] + [hbm] * 3,
+        in_specs=[vmem] * 7 + [pl.BlockSpec(memory_space=pltpu.SMEM)] * 2 + [hbm] * 3,
         out_specs=(vmem, vmem),
         scratch_shapes=[
             pltpu.VMEM((NCH, 8, feat, CH), BF16),
@@ -469,7 +455,6 @@
             pltpu.VMEM((feature_count, 512), BF16),
             pltpu.VMEM((12, CH, 512), BF16),
             pltpu.VMEM((NCH, CH, 512), BF16),
-            pltpu.VMEM((NCH, CH, 512), BF16),
             pltpu.VMEM((32, dec_rows, 512), BF16),
             pltpu.VMEM((dec_rows, 256), BF16),
             pltpu.VMEM((dec_rows, 256), BF16),
@@ -477,7 +462,10 @@
             pltpu.VMEM((NY, NZ, dec_rows, 640), BF16),
             pltpu.VMEM((NZ, dec_rows, 640), BF16),
             pltpu.VMEM((NZ, dec_rows, 640), BF16),
-            dma((6, 7)), dma((6, 7)), dma((3,)), dma((3, NCH)), dma((3, NCH)),
+            pltpu.VMEM((NCH, 2, 2 * CH, 1), F32),
+            pltpu.VMEM((NCH, 2, 2 * CH, 1), F32),
+            pltpu.VMEM((NCH, 2, 2 * CH, HD), F32),
+            dma((6, 7)), dma((6, 7)), dma((3,)), dma((2, NCH)), dma((2, NCH)),
             dma((NZ - 1,)), dma((NZ - 1,)), dma((NY - 1,)), dma((NY - 1,)),
             dma((NY - 1,)), dma((NY - 1,)), dma((NZ - 1,)), dma((NZ - 1,)),
         ],
@@ -487,18 +475,23 @@
     )(
         prompt_states.T,
         decode_states,
-        gain_column,
-        mine[None, :],
-        rows,
+        norm_gain[None, :],
         jnp.asarray(frequency)[None, :],
         jnp.asarray(sign)[None, :],
         query_gain[None, :],
         key_gain[None, :],
         prompt_lengths,
+        row_prompt,
         query_weight,
         key_weight,
         value_weight,
     )
+    return pl.pallas_call(
+        hand_over,
+        out_shape=tuple(jax.ShapeDtypeStruct(a.shape, a.dtype) for a in attended),
+        in_specs=[vmem] * 2,
+        out_specs=(vmem, vmem),
+    )(*attended)
 
 
 def solution(mesh):

time: 88.5 us -> 82.3 us (0.930)
  local copies, waits for them, and re-layouts: 6.77 us -> 1.36 us
    unnamed x2 -> x0, local copies, waits for them, and re-layouts: 3.19 us -> none
    pallas_call x1, Pallas kernels: 80.8 us -> 78.3 us  [local(): pl.pallas_call(functools.partial(kernel, float(feature_count)), out_shape...]
    pallas_call x0 -> x1, Pallas kernels: none -> 1.87 us  [local(): pl.pallas_call(hand_over, out_shape=tuple((jax.ShapeDtypeStruct(a.shape,...]
    broadcast_in_dim x3 -> x1, local copies, waits for them, and re-layouts: 2.8 us -> 1.36 us  [local(): norm_gain[None, :]]
where the time goes in v2:
time: 82.3 us; the launch traced here: 82.1 us
  Pallas kernels  80.1 us (97%)
  local copies, waits for them, and re-layouts  1.36 us (2%)
    pallas_call x1, Pallas kernels, local(): pl.pallas_call(functools.partial(kernel, float(feature_count)), out_shape...  78.3 us
    pallas_call x1, Pallas kernels, local(): pl.pallas_call(hand_over, out_shape=tuple((jax.ShapeDtypeStruct(a.shape,...  1.87 us

profile of v2, /device:TPU:1, one launch (start us, length us, event | category | flops | bytes accessed | tf_op | source)
XLA Modules:
  0.0 82.1 jit_solution(17087103064512581551)
XLA Ops:
  0.6 1.4 %broadcast_in_dim.15.gain_ref = f32[1,5376]{1,0:T(1,128)} reshape(f32[5376]{0:T(1024)} %param.14) | data formatting | bytes 43008 | tf_op jit(solution)/shard_map/broadcast_in_dim | solution.py:478
  2.0 78.3 %shard_map.131 = (bf16[512,512]{1,0:T(8,128)(2,1)}, bf16[16,512]{1,0:T(8,128)(2,1)}) custom-call(bf16[672,512]{1,0:T(8,128)(2,1)} %bitcast.3, bf16[16,672]{1,0:T(8,128)(2,1)} %xd_ref.1, f32[1,5376]{1,0:T(1,128)} %broadcast_in_dim.15.gain_ref, f32[1,128]{1,0:T(1,128)} %constant.8.freq_ref, f32[1,128]{1,0:T(1,128)} %constant.9.sgn_ref, f32[1,128]{1,0:T(1,128)} %bitcast.4, ...), custom_call_target="tpu_custom_call" | custom-call | tf_op jit(solution)/shard_map/pallas_call | solution.py:442
  80.3 1.9 %shard_map.132 = (bf16[512,512]{1,0:T(8,128)(2,1)}, bf16[16,512]{1,0:T(8,128)(2,1)}) custom-call(bf16[512,512]{1,0:T(8,128)(2,1)} %get-tuple-element.4.a_ref, bf16[16,512]{1,0:T(8,128)(2,1)} %get-tuple-element.5.b_ref), custom_call_target="tpu_custom_call" | custom-call | tf_op jit(solution)/shard_map/pallas_call | solution.py:489

commit v3 on v2

--- a/solution.py
+++ b/solution.py
@@ -15,6 +15,7 @@
 PROMPTS = 4
 EPS = 1e-06
 SCORE_SCALE = 168.0 ** (-0.5)
+LOG2_SCALE = SCORE_SCALE * math.log2(math.e)
 HD = 128
 NY, NZ, NX = 4, 8, 4
 CH = 128
@@ -31,7 +32,7 @@
     x_ref, xd_ref, gain_ref, freq_ref, sgn_ref, qg_ref, kg_ref, len_ref, rp_ref,
     wq_hbm, wk_hbm, wv_hbm,
     out_ref, dout_ref,
-    xg, xd, ss, wkv, wq, kv, q_s, dqg, dk_s, dv_s, dpart, b1, p2, b2, top_s, sum_s, mix_s,
+    xg, xd, ss, wkv, wq, kv, q_s, dqg, dk_s, dv_s, dpart, b1, p2, b2, top_s, sum_s, mix_s, gain_s,
     ag_send, ag_recv, wsem, h_send, h_recv,
     dq1_send, dq1_recv, dq2_send, dq2_recv, r1_send, r1_recv, r2_send, r2_recv,
 ):
@@ -66,17 +67,22 @@
 
     barrier = pltpu.get_barrier_semaphore()
     for device in (
-        [(me_c, t) for t in (near_a, near_b, far, partner)]
+        [(me_c, t) for t in (near_a, near_b, partner)]
         + [(ctx_of(y, z + j), me_t) for j in range(1, NZ)]
         + [(ctx_of(y + j, z), me_t) for j in range(1, NY)]
         + [(in_b1, me_t)]
     ):
         pl.semaphore_signal(barrier, inc=1, device_id=device, device_id_type=MESH)
 
-    gain_row = gain_ref[:, 0:feat]
-    for t in range(1, 8):
-        gain_row = jnp.where(me_t == t, gain_ref[:, t * feat : (t + 1) * feat], gain_row)
-    gain_column = jnp.transpose(jnp.broadcast_to(gain_row, (128, feat)))
+    gains = gain_ref.shape[0]
+    padded = jnp.concatenate([gain_ref[...], jnp.zeros((128 - gains, 128), F32)], axis=0)
+    columns_of = jnp.transpose(padded)
+    for r in range(gains):
+        gain_s[r * 128 : (r + 1) * 128] = jnp.broadcast_to(columns_of[:, r : r + 1], (128, 128))
+    gain_column = gain_s[pl.ds(pl.multiple_of(me_t * feat, 32), feat), :]
+    gain_row = jnp.transpose(
+        jnp.concatenate([gain_column, jnp.zeros((-feat % 128, 128), F32)], axis=0)
+    )[0:1, :feat]
     decode_wide = xd_ref[...].astype(F32)
     xd[me_t] = (decode_wide * gain_row).astype(BF16)
     decode_sum = jnp.sum(decode_wide * decode_wide, axis=1, keepdims=True)
@@ -86,7 +92,7 @@
         xg[k, me_t] = (wide * gain_column).astype(BF16)
         ss[me_t, k] = jnp.sum((wide * wide).reshape(feat // 8, 8, CH), axis=0)
 
-    pl.semaphore_wait(barrier, 15)
+    pl.semaphore_wait(barrier, 14)
 
     def piece(k, d):
         if isinstance(k, int) and k == 4:
@@ -105,13 +111,18 @@
     def start_own(k):
         ag(k, me_t, 0, near_b).start()
         ag(k, me_t, 1, near_a).start()
-        ag(k, me_t, 2, far).start()
         ag(k, me_t, 3, partner).start()
 
-    def gather(k):
-        for j, d in enumerate((near_a, near_b, far)):
-            ag(k, d, j, near_b).wait_recv()
-            ag(k, d, 4 + j, partner).start()
+    def take(k):
+        ag(k, near_a, 0, near_b).wait_recv()
+        ag(k, near_a, 2, near_b).start()
+        ag(k, near_a, 4, partner).start()
+        ag(k, near_b, 1, near_b).wait_recv()
+        ag(k, near_b, 5, partner).start()
+
+    def finish(k):
+        ag(k, far, 2, near_b).wait_recv()
+        ag(k, far, 6, partner).start()
         for j in range(4):
             ag(k, from_partner[j], 3 + j, near_b).wait_recv()
 
@@ -139,10 +150,13 @@
 
     qg, kg = qg_ref[...], kg_ref[...]
 
-    for k in (5, 4, 0, 1, 2, 3):
+    for k in (5, 4, 0, 1):
         start_own(k)
+    for k in (5, 4, 0):
+        take(k)
+    start_own(2)
     for k in (5, 4):
-        gather(k)
+        finish(k)
 
     for copy in weights:
         copy.wait()
@@ -192,13 +206,29 @@
         dq1(j, z, z + j).start()
 
     row_index = lax.broadcasted_iota(jnp.int32, (CH, 1), 0)
-
-    def project(s, carry):
-        gather(s)
-        states = xg[s].reshape(8 * feat, CH)
+    take(1)
+    start_own(3)
+
+    def chunk_of(s):
         sums = jnp.sum(jnp.transpose(jnp.sum(ss[:, s], axis=0)), axis=1, keepdims=True)
         inverse = lax.rsqrt(sums / feature_count + EPS)
         tables = rope_tables((block * 512 + s * CH + row_index).astype(F32))
+        return xg[s].reshape(8 * feat, CH), inverse, tables
+
+    def project_query(s, states, inverse, tables):
+        acc = dot(states, wq[...], ((0,), (0,)))
+        for h in range(4):
+            q_s[s, :, h * HD : (h + 1) * HD] = head(
+                acc[:, h * HD : (h + 1) * HD] * inverse, qg, tables
+            )
+
+    def project(s, carry):
+        @pl.when((s >= 1) & (s < NCH - 1))
+        def _():
+            take(s + 1)
+
+        finish(s)
+        states, inverse, tables = chunk_of(s)
         acc = dot(states, wkv[...], ((0,), (0,)))
         for h in range(2):
             kv[8 + s, :, h * HD : (h + 1) * HD] = head(
@@ -207,11 +237,10 @@
         kv[8 + s, :, 256:512] = (acc[:, 256:512] * inverse).astype(BF16)
         halo(0, s).start()
         halo(1, s).start()
-        acc = dot(states, wq[...], ((0,), (0,)))
-        for h in range(4):
-            q_s[s, :, h * HD : (h + 1) * HD] = head(
-                acc[:, h * HD : (h + 1) * HD] * inverse, qg, tables
-            )
+
+        @pl.when(s < NCH - 1)
+        def _():
+            project_query(s, states, inverse, tables)
 
         @pl.when(s == 1)
         def _():
@@ -231,23 +260,17 @@
     bias = jnp.where((key_pos >= length - WINDOW) & (key_pos < length), 0.0, NEG)
     lane = lax.broadcasted_iota(jnp.int32, (1, 128), 1)
 
-    def pack(lse_list):
-        packed = None
-        for h, lse in enumerate(lse_list):
-            high = lse.astype(BF16).astype(F32)
-            middle = (lse - high).astype(BF16).astype(F32)
-            low = lse - high - middle
-            term = (
-                jnp.where(lane == h, high, 0.0)
-                + jnp.where(lane == 4 + h, middle, 0.0)
-                + jnp.where(lane == 8 + h, low, 0.0)
-            )
-            packed = term if packed is None else packed + term
-        return packed.astype(BF16)
-
-    def lse_of(packed, h):
+    def pack(columns):
+        both = jnp.where(lane < 2, *[jnp.where(lane % 2 == 0, *columns[k : k + 2]) for k in (0, 2)])
+        both = jnp.where(lane < 4, both, 0.0)
+        high = both.astype(BF16).astype(F32)
+        middle = (both - high).astype(BF16).astype(F32)
+        low = both - high - middle
+        return (high + pltpu.roll(middle, 4, axis=1) + pltpu.roll(low, 8, axis=1)).astype(BF16)
+
+    def unpack(packed):
         wide = packed.astype(F32)
-        return wide[:, h : h + 1] + wide[:, 4 + h : 5 + h] + wide[:, 8 + h : 9 + h]
+        return wide + pltpu.roll(wide, 124, axis=1) + pltpu.roll(wide, 120, axis=1)
 
     queries = dqg[...].reshape(512, 512)
     keys = kv[8:12].reshape(512, 512)
@@ -257,15 +280,15 @@
         scores = dot(
             queries[:, h * HD : (h + 1) * HD], keys[:, g * HD : (g + 1) * HD], ((1,), (1,))
         )
-        scores = scores * SCORE_SCALE + bias
+        scores = scores * LOG2_SCALE + bias
         top = jnp.max(scores, axis=1, keepdims=True)
-        weights_h = jnp.exp(scores - top)
+        weights_h = jnp.exp2(scores - top)
         total = jnp.sum(weights_h, axis=1, keepdims=True)
         mixed = dot(
             weights_h.astype(BF16), keys[:, 256 + g * HD : 256 + (g + 1) * HD], ((1,), (0,))
         )
-        dpart[:, :, h * HD : (h + 1) * HD] = (mixed / total).astype(BF16).reshape(32, 16, HD)
-        lse_list.append(top + jnp.log(total))
+        dpart[:, :, h * HD : (h + 1) * HD] = (mixed * (1.0 / total)).astype(BF16).reshape(32, 16, HD)
+        lse_list.append(top + jnp.log2(total))
     dpart[:, :, 512:640] = pack(lse_list).reshape(32, 16, 128)
 
     def r1(j, slot_y, target_y):
@@ -287,6 +310,7 @@
     for j in range(1, NY):
         r1(j, y, y + j).start()
     b1[y] = dpart[pl.ds(y * NZ, NZ)]
+    project_query(NCH - 1, *chunk_of(NCH - 1))
 
     def query_of(i, g):
         return jnp.concatenate(
@@ -294,8 +318,8 @@
         )
 
     def softmax(scores, window, g):
-        top = jnp.max(scores, axis=1, keepdims=True)
-        weights_h = jnp.exp(scores - top)
+        top = jnp.max(scores, axis=1, keepdims=True) * LOG2_SCALE
+        weights_h = jnp.exp2(scores * LOG2_SCALE - top)
         total = jnp.sum(weights_h, axis=1, keepdims=True)
         values = window[:, 256 + g * HD : 256 + (g + 1) * HD]
         return top, total, dot(weights_h.astype(BF16), values, ((1,), (0,)))
@@ -312,7 +336,7 @@
         for g in range(2):
             window = kv[pl.ds(4 + i, 5)].reshape(width, 512)
             scores = dot(query_of(i, g), window[:, g * HD : (g + 1) * HD], ((1,), (1,)))
-            scores = scores * SCORE_SCALE + low
+            scores = scores + low
             scores = jnp.concatenate(
                 [
                     jnp.where(cols > rows2, scores[:, :CH], NEG),
@@ -326,20 +350,50 @@
         return carry
 
     lax.fori_loop(0, NCH, attend_first, 0)
+    for j in range(1, NY):
+        r1(j, y - j, y).wait_recv()
+
+    def merge(parts, lses):
+        top = functools.reduce(jnp.maximum, lses)
+        factors = [jnp.exp2(lse - top) for lse in lses]
+        total = sum(factors)
+        mixed = [
+            sum(
+                f[:, h : h + 1] * part[:, h * HD : (h + 1) * HD].astype(F32)
+                for f, part in zip(factors, parts)
+            )
+            for h in range(4)
+        ]
+        return top, total, mixed
+
+    parts = [b1[i].reshape(128, 640) for i in range(NY)]
+    top, total, mixed = merge(parts, [unpack(part[:, 512:640]) for part in parts])
+    share = 1.0 / total
+    for h in range(4):
+        p2[:, :, h * HD : (h + 1) * HD] = (
+            (mixed[h] * share[:, h : h + 1]).astype(BF16).reshape(8, 16, HD)
+        )
+    lse = top + jnp.log2(total)
+    p2[:, :, 512:640] = pack([lse[:, h : h + 1] for h in range(4)]).reshape(8, 16, 128)
+    for j in range(1, NZ):
+        r2(j, z, z + j).start()
+    b2[z] = p2[z]
+
     for s in range(NCH):
         halo(1, s).wait_recv()
-    absent = jnp.where(block == 0, NEG, 0.0)
 
     def attend_last(i, carry):
         alive = block * 512 + i * CH + rows2 < length
         for g in range(2):
             window = kv[0:4].reshape(512, 512)
             scores = dot(query_of(i, g), window[:, g * HD : (g + 1) * HD], ((1,), (1,)))
-            top, total, mixed = softmax(scores * SCORE_SCALE + absent, window, g)
+            top, total, mixed = softmax(scores, window, g)
+            top = jnp.where(block == 0, NEG, top)
             first_top = top_s[i, g]
             both = jnp.maximum(top, first_top)
-            f1, f2 = jnp.exp(first_top - both), jnp.exp(top - both)
-            mixed = (mix_s[i, g] * f1 + mixed * f2) / (sum_s[i, g] * f1 + total * f2)
+            f1, f2 = jnp.exp2(first_top - both), jnp.exp2(top - both)
+            share = 1.0 / (sum_s[i, g] * f1 + total * f2)
+            mixed = mix_s[i, g] * (f1 * share) + mixed * (f2 * share)
             mixed = jnp.where(alive, mixed, 0.0).astype(BF16)
             for r in range(2):
                 out_ref[
@@ -350,39 +404,17 @@
 
     lax.fori_loop(0, NCH, attend_last, 0)
 
-    for j in range(1, NY):
-        r1(j, y - j, y).wait_recv()
-
-    def merge(parts, masks, h):
-        lses = [lse_of(part[:, 512:640], h) for part in parts]
-        if masks is not None:
-            lses = [jnp.where(mask, lse, NEG) for mask, lse in zip(masks, lses)]
-        top = functools.reduce(jnp.maximum, lses)
-        factors = [jnp.exp(lse - top) for lse in lses]
-        total = sum(factors)
-        mixed = sum(
-            f * part[:, h * HD : (h + 1) * HD].astype(F32) for f, part in zip(factors, parts)
-        )
-        return top, total, mixed
-
-    parts = [b1[i].reshape(128, 640) for i in range(NY)]
-    lse_list = []
-    for h in range(4):
-        top, total, mixed = merge(parts, None, h)
-        p2[:, :, h * HD : (h + 1) * HD] = (mixed / total).astype(BF16).reshape(8, 16, HD)
-        lse_list.append(top + jnp.log(total))
-    p2[:, :, 512:640] = pack(lse_list).reshape(8, 16, 128)
-    for j in range(1, NZ):
-        r2(j, z, z + j).start()
-    b2[z] = p2[z]
     for j in range(1, NZ):
         r2(j, z - j, z).wait_recv()
     parts = [b2[i] for i in range(NZ)]
-    masks = [rp[:, :1] == i % PROMPTS for i in range(NZ)]
+    lses = [
+        jnp.where(rp == i % PROMPTS, unpack(part[:, 512:640]), NEG) for i, part in enumerate(parts)
+    ]
+    tops, totals, mixed = merge(parts, lses)
     own_query = dqg[me_c].astype(F32)
     for h in range(4):
         g = h // 2
-        top, total, mixed = merge(parts, masks, h)
+        top, total = tops[:, h : h + 1], totals[:, h : h + 1]
         own = (
             jnp.sum(
                 own_query[:, h * HD : (h + 1) * HD]
@@ -390,14 +422,14 @@
                 axis=1,
                 keepdims=True,
             )
-            * SCORE_SCALE
+            * LOG2_SCALE
         )
         new_top = jnp.maximum(top, own)
-        shift = jnp.exp(top - new_top)
-        weight = jnp.exp(own - new_top)
+        shift = jnp.exp2(top - new_top)
+        weight = jnp.exp2(own - new_top)
         value = dv_s[:, g * HD : (g + 1) * HD].astype(F32)
         dout_ref[:, h * HD : (h + 1) * HD] = (
-            (mixed * shift + weight * value) / (total * shift + weight)
+            (mixed[h] * shift + weight * value) / (total * shift + weight)
         ).astype(BF16)
 
     for k in range(6):
@@ -465,6 +497,7 @@
             pltpu.VMEM((NCH, 2, 2 * CH, 1), F32),
             pltpu.VMEM((NCH, 2, 2 * CH, 1), F32),
             pltpu.VMEM((NCH, 2, 2 * CH, HD), F32),
+            pltpu.VMEM((feature_count, 128), F32),
             dma((6, 7)), dma((6, 7)), dma((3,)), dma((2, NCH)), dma((2, NCH)),
             dma((NZ - 1,)), dma((NZ - 1,)), dma((NY - 1,)), dma((NY - 1,)),
             dma((NY - 1,)), dma((NY - 1,)), dma((NZ - 1,)), dma((NZ - 1,)),
@@ -475,7 +508,7 @@
     )(
         prompt_states.T,
         decode_states,
-        norm_gain[None, :],
+        norm_gain.reshape(-1, 128),
         jnp.asarray(frequency)[None, :],
         jnp.asarray(sign)[None, :],
         query_gain[None, :],

time: 82.3 us -> 79.7 us (0.968)
  local copies, waits for them, and re-layouts: 1.36 us -> 0 us
  Pallas kernels: 80.1 us -> 79 us
    broadcast_in_dim x1 -> x0, local copies, waits for them, and re-layouts: 1.36 us -> none  [local(): norm_gain[None, :]]
    pallas_call x1, Pallas kernels: 78.3 us -> 77.1 us  [local(): pl.pallas_call(functools.partial(kernel, float(feature_count)), out_shape...]
where the time goes in v3:
time: 79.7 us; the launch traced here: 79.6 us
  Pallas kernels  79 us (99%)
    pallas_call x1, Pallas kernels, local(): pl.pallas_call(functools.partial(kernel, float(feature_count)), out_shape...  77.1 us
    pallas_call x1, Pallas kernels, local(): pl.pallas_call(hand_over, out_shape=tuple((jax.ShapeDtypeStruct(a.shape,...  1.87 us

profile of v3, /device:TPU:1, one launch (start us, length us, event | category | flops | bytes accessed | tf_op | source)
XLA Modules:
  0.0 79.6 jit_solution(11927946326618219904)
XLA Ops:
  0.6 77.1 %shard_map.131 = (bf16[512,512]{1,0:T(8,128)(2,1)}, bf16[16,512]{1,0:T(8,128)(2,1)}) custom-call(bf16[672,512]{1,0:T(8,128)(2,1)} %bitcast.4, bf16[16,672]{1,0:T(8,128)(2,1)} %xd_ref.1, f32[42,128]{1,0:T(8,128)} %bitcast.5, f32[1,128]{1,0:T(1,128)} %constant.8.freq_ref, f32[1,128]{1,0:T(1,128)} %constant.9.sgn_ref, f32[1,128]{1,0:T(1,128)} %bitcast.6, ...), custom_call_target="tpu_custom_call" | custom-call | tf_op jit(solution)/shard_map/pallas_call | solution.py:474
  77.7 1.9 %shard_map.132 = (bf16[512,512]{1,0:T(8,128)(2,1)}, bf16[16,512]{1,0:T(8,128)(2,1)}) custom-call(bf16[512,512]{1,0:T(8,128)(2,1)} %get-tuple-element.4.a_ref, bf16[16,512]{1,0:T(8,128)(2,1)} %get-tuple-element.5.b_ref), custom_call_target="tpu_custom_call" | custom-call | tf_op jit(solution)/shard_map/pallas_call | solution.py:522

commit v4 on v3

--- a/solution.py
+++ b/solution.py
@@ -89,17 +89,17 @@
     ss[me_t, 4:6] = jnp.broadcast_to(decode_sum, (16, 128)).reshape(2, 8, 128)
     for k in range(NCH):
         wide = x_ref[:, k * CH : (k + 1) * CH].astype(F32)
-        xg[k, me_t] = (wide * gain_column).astype(BF16)
+        xg[k, me_t] = (wide * gain_column).astype(BF16).reshape(2, feat // 2, CH)
         ss[me_t, k] = jnp.sum((wide * wide).reshape(feat // 8, 8, CH), axis=0)
 
     pl.semaphore_wait(barrier, 14)
 
     def piece(k, d):
-        if isinstance(k, int) and k == 4:
+        if isinstance(k, int) and k == 8:
             return xd.at[d]
-        if isinstance(k, int) and k == 5:
+        if isinstance(k, int) and k == 9:
             return ss.at[d]
-        return xg.at[k, d]
+        return xg.at[lax.div(k, 2), d, lax.rem(k, 2)]
 
     def ag(k, d, j, target):
         return pltpu.make_async_remote_copy(
@@ -150,22 +150,15 @@
 
     qg, kg = qg_ref[...], kg_ref[...]
 
-    for k in (5, 4, 0, 1):
+    for k in (9, 8, 0, 1):
         start_own(k)
-    for k in (5, 4, 0):
+    for k in (9, 8, 0, 1):
         take(k)
-    start_own(2)
-    for k in (5, 4):
+    for k in (2, 3):
+        start_own(k)
+    for k in (9, 8):
         finish(k)
 
-    for copy in weights:
-        copy.wait()
-    acc_kv = jnp.zeros((16, 512), F32)
-    acc_q = jnp.zeros((16, 512), F32)
-    for d in range(8):
-        rows = slice(d * feat, (d + 1) * feat)
-        acc_kv += dot(xd[d], wkv[rows, :], ((1,), (0,)))
-        acc_q += dot(xd[d], wq[rows, :], ((1,), (0,)))
     rows16 = lax.broadcasted_iota(jnp.int32, (16, 128), 0)
     rp = jnp.zeros((16, 128), jnp.int32)
     for r in range(16):
@@ -173,21 +166,6 @@
     decode_pos = jnp.zeros((16, 128), jnp.int32)
     for p in range(PROMPTS):
         decode_pos = jnp.where(rp == p, len_ref[p], decode_pos)
-    tables = rope_tables(decode_pos.astype(F32))
-    sums = jnp.sum(ss[:, 4:6], axis=0).reshape(16, 128)
-    inverse = lax.rsqrt(sums / feature_count + EPS)
-    for h in range(4):
-        dqg[me_c, :, h * HD : (h + 1) * HD] = head(
-            acc_q[:, h * HD : (h + 1) * HD] * inverse, qg, tables
-        )
-    for h in range(2):
-        dk_s[:, h * HD : (h + 1) * HD] = head(
-            acc_kv[:, h * HD : (h + 1) * HD] * inverse, kg, tables
-        )
-        dv_s[:, h * HD : (h + 1) * HD] = (
-            acc_kv[:, 256 + h * HD : 256 + (h + 1) * HD] * inverse
-        ).astype(BF16)
-
     def dq1(j, owner_z, target_z):
         slot = dqg.at[ctx_of(y, owner_z)]
         return pltpu.make_async_remote_copy(
@@ -202,12 +180,35 @@
             device_id=(ctx_of(target_y, z), me_t), device_id_type=MESH,
         )
 
-    for j in range(1, NZ):
-        dq1(j, z, z + j).start()
+
+    def project_decode():
+        acc_kv = jnp.zeros((16, 512), F32)
+        acc_q = jnp.zeros((16, 512), F32)
+        for d in range(8):
+            rows = slice(d * feat, (d + 1) * feat)
+            acc_kv += dot(xd[d], wkv[rows, :], ((1,), (0,)))
+            acc_q += dot(xd[d], wq[rows, :], ((1,), (0,)))
+        tables = rope_tables(decode_pos.astype(F32))
+        sums = jnp.sum(ss[:, 4:6], axis=0).reshape(16, 128)
+        inverse = lax.rsqrt(sums / feature_count + EPS)
+        for h in range(4):
+            dqg[me_c, :, h * HD : (h + 1) * HD] = head(
+                acc_q[:, h * HD : (h + 1) * HD] * inverse, qg, tables
+            )
+        for h in range(2):
+            dk_s[:, h * HD : (h + 1) * HD] = head(
+                acc_kv[:, h * HD : (h + 1) * HD] * inverse, kg, tables
+            )
+            dv_s[:, h * HD : (h + 1) * HD] = (
+                acc_kv[:, 256 + h * HD : 256 + (h + 1) * HD] * inverse
+            ).astype(BF16)
+
+        for j in range(1, NZ):
+            dq1(j, z, z + j).start()
 
     row_index = lax.broadcasted_iota(jnp.int32, (CH, 1), 0)
-    take(1)
-    start_own(3)
+    weights[0].wait()
+    weights[1].wait()
 
     def chunk_of(s):
         sums = jnp.sum(jnp.transpose(jnp.sum(ss[:, s], axis=0)), axis=1, keepdims=True)
@@ -223,11 +224,8 @@
             )
 
     def project(s, carry):
-        @pl.when((s >= 1) & (s < NCH - 1))
-        def _():
-            take(s + 1)
-
-        finish(s)
+        finish(2 * s)
+        finish(2 * s + 1)
         states, inverse, tables = chunk_of(s)
         acc = dot(states, wkv[...], ((0,), (0,)))
         for h in range(2):
@@ -237,6 +235,21 @@
         kv[8 + s, :, 256:512] = (acc[:, 256:512] * inverse).astype(BF16)
         halo(0, s).start()
         halo(1, s).start()
+
+        @pl.when(s < NCH - 1)
+        def _():
+            take(2 * s + 2)
+            take(2 * s + 3)
+
+        @pl.when(s < NCH - 2)
+        def _():
+            start_own(2 * s + 4)
+            start_own(2 * s + 5)
+
+        @pl.when(s == 0)
+        def _():
+            weights[2].wait()
+            project_decode()
 
         @pl.when(s < NCH - 1)
         def _():
@@ -272,6 +285,18 @@
         wide = packed.astype(F32)
         return wide + pltpu.roll(wide, 124, axis=1) + pltpu.roll(wide, 120, axis=1)
 
+    def r1(j, slot_y, target_y):
+        return pltpu.make_async_remote_copy(
+            src_ref=dpart.at[pl.ds(lax.rem(target_y + NY, NY) * NZ, NZ)],
+            dst_ref=b1.at[lax.rem(slot_y + NY, NY)],
+            send_sem=r1_send.at[j - 1], recv_sem=r1_recv.at[j - 1],
+            device_id=(ctx_of(target_y, z), me_t), device_id_type=MESH,
+        )
+
+    def send_parts():
+        for j in range(1, NY):
+            r1(j, y, y + j).start()
+
     queries = dqg[...].reshape(512, 512)
     keys = kv[8:12].reshape(512, 512)
     lse_list = []
@@ -290,14 +315,7 @@
         dpart[:, :, h * HD : (h + 1) * HD] = (mixed * (1.0 / total)).astype(BF16).reshape(32, 16, HD)
         lse_list.append(top + jnp.log2(total))
     dpart[:, :, 512:640] = pack(lse_list).reshape(32, 16, 128)
-
-    def r1(j, slot_y, target_y):
-        return pltpu.make_async_remote_copy(
-            src_ref=dpart.at[pl.ds(lax.rem(target_y + NY, NY) * NZ, NZ)],
-            dst_ref=b1.at[lax.rem(slot_y + NY, NY)],
-            send_sem=r1_send.at[j - 1], recv_sem=r1_recv.at[j - 1],
-            device_id=(ctx_of(target_y, z), me_t), device_id_type=MESH,
-        )
+    send_parts()
 
     def r2(j, slot_z, target_z):
         return pltpu.make_async_remote_copy(
@@ -307,8 +325,6 @@
             device_id=(ctx_of(y, target_z), me_t), device_id_type=MESH,
         )
 
-    for j in range(1, NY):
-        r1(j, y, y + j).start()
     b1[y] = dpart[pl.ds(y * NZ, NZ)]
     project_query(NCH - 1, *chunk_of(NCH - 1))
 
@@ -353,21 +369,22 @@
     for j in range(1, NY):
         r1(j, y - j, y).wait_recv()
 
-    def merge(parts, lses):
+    def merge(part_of, count, lses):
         top = functools.reduce(jnp.maximum, lses)
         factors = [jnp.exp2(lse - top) for lse in lses]
         total = sum(factors)
         mixed = [
             sum(
-                f[:, h : h + 1] * part[:, h * HD : (h + 1) * HD].astype(F32)
-                for f, part in zip(factors, parts)
+                factors[i][:, h : h + 1] * part_of(i, h).astype(F32) for i in range(count)
             )
             for h in range(4)
         ]
         return top, total, mixed
 
-    parts = [b1[i].reshape(128, 640) for i in range(NY)]
-    top, total, mixed = merge(parts, [unpack(part[:, 512:640]) for part in parts])
+    def over_y(i, h):
+        return b1[i, :, :, h * HD : (h + 1) * HD].reshape(128, HD)
+
+    top, total, mixed = merge(over_y, NY, [unpack(over_y(i, 4)) for i in range(NY)])
     share = 1.0 / total
     for h in range(4):
         p2[:, :, h * HD : (h + 1) * HD] = (
@@ -406,11 +423,11 @@
 
     for j in range(1, NZ):
         r2(j, z - j, z).wait_recv()
-    parts = [b2[i] for i in range(NZ)]
-    lses = [
-        jnp.where(rp == i % PROMPTS, unpack(part[:, 512:640]), NEG) for i, part in enumerate(parts)
-    ]
-    tops, totals, mixed = merge(parts, lses)
+    def over_z(i, h):
+        return b2[i, :, h * HD : (h + 1) * HD]
+
+    lses = [jnp.where(rp == i % PROMPTS, unpack(over_z(i, 4)), NEG) for i in range(NZ)]
+    tops, totals, mixed = merge(over_z, NZ, lses)
     own_query = dqg[me_c].astype(F32)
     for h in range(4):
         g = h // 2
@@ -432,7 +449,7 @@
             (mixed[h] * shift + weight * value) / (total * shift + weight)
         ).astype(BF16)
 
-    for k in range(6):
+    for k in range(10):
         ag_sent(k)
     for s in range(NCH):
         for kind in range(2):
@@ -480,7 +497,7 @@
         in_specs=[vmem] * 7 + [pl.BlockSpec(memory_space=pltpu.SMEM)] * 2 + [hbm] * 3,
         out_specs=(vmem, vmem),
         scratch_shapes=[
-            pltpu.VMEM((NCH, 8, feat, CH), BF16),
+            pltpu.VMEM((NCH, 8, 2, feat // 2, CH), BF16),
             pltpu.VMEM((8, dec_rows, feat), BF16),
             pltpu.VMEM((8, 6, 8, 128), F32),
             pltpu.VMEM((feature_count, 512), BF16),
@@ -498,7 +515,7 @@
             pltpu.VMEM((NCH, 2, 2 * CH, 1), F32),
             pltpu.VMEM((NCH, 2, 2 * CH, HD), F32),
             pltpu.VMEM((feature_count, 128), F32),
-            dma((6, 7)), dma((6, 7)), dma((3,)), dma((2, NCH)), dma((2, NCH)),
+            dma((10, 7)), dma((10, 7)), dma((3,)), dma((2, NCH)), dma((2, NCH)),
             dma((NZ - 1,)), dma((NZ - 1,)), dma((NY - 1,)), dma((NY - 1,)),
             dma((NY - 1,)), dma((NY - 1,)), dma((NZ - 1,)), dma((NZ - 1,)),
         ],

time: 79.7 us -> 76.8 us (0.964)
  Pallas kernels: 79 us -> 76.1 us
    pallas_call x1, Pallas kernels: 77.1 us -> 74.2 us  [local(): pl.pallas_call(functools.partial(kernel, float(feature_count)), out_shape...]
where the time goes in v4:
time: 76.8 us; the launch traced here: 76.7 us
  Pallas kernels  76.1 us (99%)
    pallas_call x1, Pallas kernels, local(): pl.pallas_call(functools.partial(kernel, float(feature_count)), out_shape...  74.2 us
    pallas_call x1, Pallas kernels, local(): pl.pallas_call(hand_over, out_shape=tuple((jax.ShapeDtypeStruct(a.shape,...  1.87 us

profile of v4, /device:TPU:1, one launch (start us, length us, event | category | flops | bytes accessed | tf_op | source)
XLA Modules:
  0.0 76.7 jit_solution(17511808483286921858)
XLA Ops:
  0.6 74.2 %shard_map.131 = (bf16[512,512]{1,0:T(8,128)(2,1)}, bf16[16,512]{1,0:T(8,128)(2,1)}) custom-call(bf16[672,512]{1,0:T(8,128)(2,1)} %bitcast.4, bf16[16,672]{1,0:T(8,128)(2,1)} %xd_ref.1, f32[42,128]{1,0:T(8,128)} %bitcast.5, f32[1,128]{1,0:T(1,128)} %constant.8.freq_ref, f32[1,128]{1,0:T(1,128)} %constant.9.sgn_ref, f32[1,128]{1,0:T(1,128)} %bitcast.6, ...), custom_call_target="tpu_custom_call" | custom-call | tf_op jit(solution)/shard_map/pallas_call | solution.py:491
  74.8 1.9 %shard_map.132 = (bf16[512,512]{1,0:T(8,128)(2,1)}, bf16[16,512]{1,0:T(8,128)(2,1)}) custom-call(bf16[512,512]{1,0:T(8,128)(2,1)} %get-tuple-element.4.a_ref, bf16[16,512]{1,0:T(8,128)(2,1)} %get-tuple-element.5.b_ref), custom_call_target="tpu_custom_call" | custom-call | tf_op jit(solution)/shard_map/pallas_call | solution.py:539
